TPU v7x, 32 devices: a whole 2x2x4 slice. The times are simulated.
32 devices in a mesh: grp: 4 (over y, core), inner: 8 (over z, x).
Axes of the slice: x: 2, y: 2, z: 4, core: 2. Of those that a mesh axis runs over, the one named last changes fastest.
Arguments:
- grad_out: bfloat16 [4096, 2048], P(('grp', 'inner')), may hold values from -6 to 6
- hidden: bfloat16 [4096, 2048], P(('grp', 'inner')), may hold values from -6 to 6
- norm_gain: float32 [2048], replicated, may hold values from 0.25 to 1.75
- expert_ids: int32 [4096, 8], P(('grp', 'inner')), may hold values from 0 to 31, all different within a row; in each aligned block of 128 rows (0 to 127, 128 to 255, ...) at most 40 rows name the same one
- gate_weights: float32 [4096, 8], P(('grp', 'inner')), may hold values from 0.02 to 0.5
- w_gate: bfloat16 [32, 2048, 768], P(('grp', 'inner')), may hold values from -0.125 to 0.125
- w_up: bfloat16 [32, 2048, 768], P(('grp', 'inner')), may hold values from -0.125 to 0.125
- w_down: bfloat16 [32, 768, 2048], P(('grp', 'inner')), may hold values from -0.21875 to 0.21875
- w_out: bfloat16 [4096, 2048], P('inner'), may hold values from -0.09375 to 0.09375
- queries: bfloat16 [4096, 4096], P(('grp', 'inner')), may hold values from -0.6 to 0.6
- keys: bfloat16 [4096, 512], P(('grp', 'inner')), may hold values from -0.6 to 0.6
- values: bfloat16 [4096, 512], P(('grp', 'inner')), may hold values from -6 to 6
- attn_out: bfloat16 [4096, 4096], P(('grp', 'inner')), may hold values from -6 to 6
- lse: float32 [32, 4096], P('inner', 'grp'), as said below
Outputs:
- grad_resid: bfloat16 [4096, 2048], P(('grp', 'inner'))
- queries_gradient: bfloat16 [4096, 4096], P(('grp', 'inner'))
- keys_gradient: bfloat16 [4096, 512], P(('grp', 'inner'))
- values_gradient: bfloat16 [4096, 512], P(('grp', 'inner'))
Inputs may be any that keep to these rules, and one draw needn't show every extreme that they name: `expert_ids`: each token names 8 different experts. Among the 128 tokens of one device (aligned blocks of rows), no expert is named by more than 40 tokens; in some device's tokens one expert is named by exactly 40. lse[h, t] minus log(1 + the position of token t in its sequence of 1024) lies between 0 and 1.5.
All inputs are finite; a program needn't handle non-finite values.
Results may differ from a plain program's by a relative error of at most 0.012.
Values may be sent and summed in bfloat16 or wider, within the bound.
A program may use at most 192 MiB of HBM per device.

v0:
```python
import jax
import jax.numpy as jnp
from jax import lax
from jax.sharding import PartitionSpec as P

KEY_VALUE_HEADS = 4
HEAD_SIZE = 128


EPSILON = 1e-06


def contract_last(left, right):
    return lax.dot_general(
        left, right, (((1,), (1,)), ((), ())), preferred_element_type=jnp.float32
    )


def contract_first(left, right):
    return lax.dot_general(
        left, right, (((0,), (0,)), ((), ())), preferred_element_type=jnp.float32
    )


def expert_grads(received, w_gate, w_up, w_down):
    local = w_gate.shape[0]
    width = w_gate.shape[1]
    shaped = received.reshape((-1, local) + received.shape[1:])
    inputs = shaped[..., :width]
    upstream = shaped[..., width:]
    gate_pre = jnp.einsum("nlcd,ldf->nlcf", inputs, w_gate, preferred_element_type=jnp.float32)
    up_pre = jnp.einsum("nlcd,ldf->nlcf", inputs, w_up, preferred_element_type=jnp.float32)
    back_hidden = jnp.einsum("nlcd,lfd->nlcf", upstream, w_down, preferred_element_type=jnp.float32)
    sigmoid = jax.nn.sigmoid(gate_pre)
    grad_gate = (back_hidden * up_pre * sigmoid * (1.0 + gate_pre * (1.0 - sigmoid))).astype(
        jnp.bfloat16
    )
    grad_up = (back_hidden * gate_pre * sigmoid).astype(jnp.bfloat16)
    grad_in = jnp.einsum("nlcf,ldf->nlcd", grad_gate, w_gate, preferred_element_type=jnp.float32)
    grad_in = grad_in + jnp.einsum(
        "nlcf,ldf->nlcd", grad_up, w_up, preferred_element_type=jnp.float32
    )
    return grad_in.astype(jnp.bfloat16).reshape(received.shape[:-1] + (width,))


def per_device(
    grad_out,
    hidden,
    norm_gain,
    expert_ids,
    gate_weights,
    w_gate,
    w_up,
    w_down,
    w_out,
    queries,
    keys,
    values,
    attn_out,
    lse,
):
    token_rows, width = hidden.shape
    topk = expert_ids.shape[1]
    groups = lax.axis_size("grp")
    inner_product = lax.axis_size("inner")
    experts_all = w_gate.shape[0] * groups * inner_product
    capacity = max(2, 5 * token_rows * topk // (4 * experts_all))
    hidden_f = hidden.astype(jnp.float32)
    inverse = lax.rsqrt(jnp.mean(hidden_f * hidden_f, axis=1, keepdims=True) + EPSILON)
    normed = (hidden_f * inverse * norm_gain).astype(jnp.bfloat16)
    upstream = grad_out.astype(jnp.float32)
    flat_count = token_rows * topk
    flat_ids = expert_ids.reshape(-1)
    one_hot = (flat_ids[:, None] == jnp.arange(experts_all, dtype=jnp.int32)[None, :]).astype(
        jnp.int32
    )
    slot_rank = jnp.sum((jnp.cumsum(one_hot, axis=0) - one_hot) * one_hot, axis=1)
    target = flat_ids * capacity + slot_rank
    owner = (
        jnp.full((experts_all * capacity,), flat_count, jnp.int32)
        .at[target]
        .set(jnp.arange(flat_count, dtype=jnp.int32))
    )
    source_tok = owner // topk
    scaled = (
        (upstream[:, None, :] * gate_weights[:, :, None])
        .reshape(flat_count, width)
        .astype(jnp.bfloat16)
    )
    zero_row = jnp.zeros((1, width), jnp.bfloat16)
    slot_inputs = jnp.concatenate([normed, zero_row], axis=0)[source_tok]
    slot_grads = jnp.concatenate([scaled, zero_row], axis=0)[owner]
    outgoing = jnp.concatenate([slot_inputs, slot_grads], axis=1).reshape(
        experts_all, capacity, 2 * width
    )
    returned = lax.all_to_all(
        expert_grads(
            lax.all_to_all(outgoing, ("grp", "inner"), split_axis=0, concat_axis=0, tiled=True),
            w_gate,
            w_up,
            w_down,
        ),
        ("grp", "inner"),
        split_axis=0,
        concat_axis=0,
        tiled=True,
    )
    expert_rows = returned.reshape(-1, width)[target].astype(jnp.float32)
    grad_normed = jnp.sum(expert_rows.reshape(token_rows, topk, width), axis=1)
    gained = grad_normed * norm_gain
    statistic = jnp.mean(gained * hidden_f, axis=1, keepdims=True)
    grad_resid = (
        upstream + inverse * gained - hidden_f * inverse * inverse * inverse * statistic
    ).astype(jnp.bfloat16)
    head_width = queries.shape[1] // inner_product
    per_head = head_width // HEAD_SIZE
    shared_portion = inner_product // KEY_VALUE_HEADS
    key_value_pairs = jnp.concatenate(
        [
            keys.reshape(token_rows, KEY_VALUE_HEADS, 1, HEAD_SIZE),
            values.reshape(token_rows, KEY_VALUE_HEADS, 1, HEAD_SIZE),
        ],
        axis=2,
    )
    key_value_broadcast = jnp.broadcast_to(
        key_value_pairs[:, :, None], (token_rows, KEY_VALUE_HEADS, shared_portion, 2, HEAD_SIZE)
    ).reshape(token_rows, inner_product * 2 * HEAD_SIZE)
    head_query, head_output, head_kv = (
        lax.all_to_all(queries, "inner", split_axis=1, concat_axis=0, tiled=True),
        lax.all_to_all(attn_out, "inner", split_axis=1, concat_axis=0, tiled=True),
        lax.all_to_all(key_value_broadcast, "inner", split_axis=1, concat_axis=0, tiled=True),
    )
    head_grad = contract_last(
        lax.all_gather(grad_resid, "inner", axis=0, tiled=True), w_out
    ).astype(jnp.bfloat16)
    seq_len = head_query.shape[0]
    head_key = head_kv[:, :HEAD_SIZE]
    head_value = head_kv[:, HEAD_SIZE:]
    lse_rows = lse.T
    scale = float(HEAD_SIZE) ** (-0.5)
    blocks = 1
    while blocks < 8 and seq_len % (2 * blocks) == 0 and (seq_len // (2 * blocks) >= 512):
        blocks = blocks * 2
    block_len = seq_len // blocks
    grad_key_acc = jnp.zeros((seq_len, HEAD_SIZE), jnp.float32)
    grad_value_acc = jnp.zeros((seq_len, HEAD_SIZE), jnp.float32)
    query_parts = []
    for block_index in range(blocks):
        low = block_index * block_len
        high = low + block_len
        block_query = head_query[low:high].reshape(block_len * per_head, HEAD_SIZE)
        block_output = head_output[low:high].reshape(block_len * per_head, HEAD_SIZE)
        block_grad = head_grad[low:high].reshape(block_len * per_head, HEAD_SIZE)
        block_lse = lse_rows[low:high].reshape(-1)
        seen_key = head_key[:high]
        seen_value = head_value[:high]
        scores = contract_last(block_query, seen_key) * scale
        row_position = low + jnp.arange(block_len * per_head, dtype=jnp.int32) // per_head
        visible = jnp.arange(high, dtype=jnp.int32)[None, :] <= row_position[:, None]
        probs = jnp.where(visible, jnp.exp(scores - block_lse[:, None]), 0.0)
        grad_probs = contract_last(block_grad, seen_value)
        delta = jnp.sum(
            block_grad.astype(jnp.float32) * block_output.astype(jnp.float32), axis=1, keepdims=True
        )
        grad_scores = (probs * (grad_probs - delta)).astype(jnp.bfloat16)
        query_part = jnp.dot(grad_scores, seen_key, preferred_element_type=jnp.float32) * scale
        query_parts.append(query_part.reshape(block_len, head_width))
        grad_key_acc = grad_key_acc.at[:high].add(contract_first(grad_scores, block_query) * scale)
        grad_value_acc = grad_value_acc.at[:high].add(
            contract_first(probs.astype(jnp.bfloat16), block_grad)
        )
    grad_query_heads = jnp.concatenate(query_parts, axis=0)
    kv_heads = jnp.concatenate([grad_key_acc, grad_value_acc], axis=1)
    token_query, token_key_value = (
        lax.all_to_all(
            grad_query_heads.astype(jnp.bfloat16), "inner", split_axis=0, concat_axis=1, tiled=True
        ).astype(grad_query_heads.dtype),
        lax.all_to_all(
            kv_heads.astype(jnp.bfloat16), "inner", split_axis=0, concat_axis=1, tiled=True
        ).astype(kv_heads.dtype),
    )
    summed_total = jnp.sum(
        token_key_value.reshape(token_rows, KEY_VALUE_HEADS, shared_portion, 2, HEAD_SIZE), axis=2
    )
    keys_gradient = (
        summed_total[:, :, 0].reshape(token_rows, KEY_VALUE_HEADS * HEAD_SIZE).astype(jnp.bfloat16)
    )
    values_gradient = (
        summed_total[:, :, 1].reshape(token_rows, KEY_VALUE_HEADS * HEAD_SIZE).astype(jnp.bfloat16)
    )
    return (grad_resid, token_query.astype(jnp.bfloat16), keys_gradient, values_gradient)


def solution(mesh):
    placed = (
        P(("grp", "inner"), None),
        P(("grp", "inner"), None),
        P(),
        P(("grp", "inner"), None),
        P(("grp", "inner"), None),
        P(("grp", "inner"), None, None),
        P(("grp", "inner"), None, None),
        P(("grp", "inner"), None, None),
        P("inner", None),
        P(("grp", "inner"), None),
        P(("grp", "inner"), None),
        P(("grp", "inner"), None),
        P(("grp", "inner"), None),
        P("inner", "grp"),
    )
    return jax.shard_map(
        per_device,
        mesh=mesh,
        in_specs=placed,
        out_specs=(
            P(("grp", "inner"), None),
            P(("grp", "inner"), None),
            P(("grp", "inner"), None),
            P(("grp", "inner"), None),
        ),
        check_vma=False,
    )
```

profile of v0, /device:TPU:0, one launch (start us, length us, event | category | flops | bytes accessed | tf_op | source)
XLA Modules:
  0.0 703.7 jit_solution(6819157236707091354)
XLA Ops:
  9.0 9.0 %reduce-window.6 = s32[32,8,128]{2,1,0:T(8,128)S(1)} reduce-window(s32[32,8,128]{2,1,0:T(8,128)S(1)} %fusion.59, s32[]{:T(128)} %constant.175.clone.1), window={size=1x1x128 pad=0_0x0_0x127_0}, to_apply=%region_1.0 | reduce-window | flops 4161536 | bytes 262148 | tf_op jit(solution)/shard_map/reduce-window
  18.8 4.3 scatter_custom_fusion
  31.4 2.4 concatenate.36
  33.8 12.0 %gather_fusion = bf16[1280,2048]{1,0:T(8,128)(2,1)} fusion(bf16[129,2048]{1,0:T(8,128)(2,1)} %concatenate.35, s32[2048]{0:T(1024)S(1)} %get-tuple-element.85), kind=kCustom, calls=%fused_computation | custom fusion | bytes 10490880 | tf_op jit(solution)/shard_map/gather | solution.py:91
  45.8 13.6 %gather_fusion.1 = bf16[1280,2048]{1,0:T(8,128)(2,1)} fusion(bf16[1025,2048]{1,0:T(8,128)(2,1)} %concatenate.36, s32[2048]{0:T(1024)S(1)} %get-tuple-element.84), kind=kCustom, calls=%fused_computation.1 | custom fusion | bytes 10490880 | tf_op jit(solution)/shard_map/gather | solution.py:92
  59.3 5.6 pad_maximum_fusion
  64.9 237.3 %all_to_all.87 = bf16[32,40,4096]{2,1,0:T(8,128)(2,1)S(1)} all-to-all(bf16[32,40,4096]{2,1,0:T(8,128)(2,1)S(1)} %bitcast.178), channel_id=1, replica_groups=mesh['grp'=4,'inner'=8] {'grp','inner'}, dimensions={0} | all-to-all | bytes 20971520 | tf_op jit(solution)/shard_map/all_to_all | solution.py:98
  302.2 6.3 fusion.2
  308.6 6.3 fusion.3
  314.9 16.7 %fusion.16 = f32[32,40,2048]{2,1,0:T(8,128)} fusion(bf16[1,2048,768]{2,1,0:T(8,128)(2,1)} %param.31, f32[32,40,768]{2,1,0:T(8,128)} %fusion.2, f32[32,40,768]{2,1,0:T(8,128)} %fusion.3, bf16[32,1,40,4096]{3,2,0,1:T(8,128)(2,1)} %bitcast.183, bf16[1,2048,768]{2,1,0:T(8,128)(2,1)S(1)} %copy-done), kind=kOutput, calls=%fused_computation.35 | convolution fusion | flops 8062894080 | bytes 29884416 | tf_op jit(solution)/shard_map/nlcf,ldf->nlcd/dot_general | solution.py:39
  331.6 11.4 %add_convert_fusion = bf16[32,40,2048]{2,1,0:T(8,128)(2,1)} fusion(f32[32,40,2048]{2,1,0:T(8,128)} %fusion.16, bf16[1,2048,768]{2,1,0:T(8,128)(2,1)S(1)} %copy-done, f32[32,40,768]{2,1,0:T(8,128)} %fusion.2, f32[32,40,768]{2,1,0:T(8,128)} %fusion.3), kind=kOutput, calls=%fused_computation.5 | convolution fusion | flops 4037672960 | bytes 26738688 | tf_op jit(solution)/shard_map/nlcf,ldf->nlcd/dot_general | solution.py:40
  343.0 3.6 all-to-all-start.1
  346.6 117.5 %all-to-all-done.1 = bf16[32,40,2048]{2,1,0:T(8,128)(2,1)} async-done(((bf16[32,40,2048]{2,1,0:T(8,128)(2,1)}), bf16[32,40,2048]{2,1,0:T(8,128)(2,1)}, u32[]{:S(2)}, u32[]{:S(2)}) %all-to-all-start.1) | async-done | bytes 5242912 | tf_op jit(solution)/shard_map/all_to_all | solution.py:96
  464.1 12.0 %gather_fusion.2 = bf16[1024,2048]{1,0:T(8,128)(2,1)} fusion(bf16[1280,2048]{1,0:T(8,128)(2,1)} %bitcast.30, s32[1024]{0:T(1024)S(1)} %broadcast_clamp_fusion), kind=kCustom, calls=%fused_computation.2 | custom fusion | bytes 8392704 | tf_op jit(solution)/shard_map/gather | solution.py:108
  476.1 5.2 convert_reduce_fusion
  484.8 3.6 all-to-all-start.4
  489.5 41.6 %all-to-all-done.4 = bf16[128,8,512]{2,0,1:T(8,128)(2,1)S(1)} async-done(((bf16[128,8,512]{2,0,1:T(8,128)(2,1)}), bf16[128,8,512]{2,0,1:T(8,128)(2,1)S(1)}, u32[]{:S(2)}, u32[]{:S(2)}) %all-to-all-start.4) | async-done | bytes 1048608 | tf_op jit(solution)/shard_map/all_to_all | solution.py:130
  531.1 3.6 all-to-all-start.3
  536.7 51.5 %all-to-all-done.3 = bf16[128,8,512]{2,0,1:T(8,128)(2,1)S(1)} async-done(((bf16[128,8,512]{2,0,1:T(8,128)(2,1)}), bf16[128,8,512]{2,0,1:T(8,128)(2,1)S(1)}, u32[]{:S(2)}, u32[]{:S(2)}) %all-to-all-start.3) | async-done | bytes 1048608 | tf_op jit(solution)/shard_map/all_to_all | solution.py:129
  588.2 4.4 all-to-all-start.2
  598.5 8.1 %all-to-all-done.2 = bf16[128,8,256]{2,0,1:T(8,128)(2,1)} async-done(((bf16[128,8,256]{2,0,1:T(8,128)(2,1)}), bf16[128,8,256]{2,0,1:T(8,128)(2,1)}, u32[]{:S(2)}, u32[]{:S(2)}) %all-to-all-start.2) | async-done | bytes 524320 | tf_op jit(solution)/shard_map/all_to_all | solution.py:131
  606.6 4.0 bitcast_select_fusion.1
  610.6 5.4 fusion.53
  616.0 5.2 convolution_convert_fusion
  622.8 3.1 fusion.24
  632.8 6.5 multiply_convert_fusion
  643.9 4.2 all-to-all-start.6
  650.0 3.5 fusion.23
  654.9 7.3 %all-to-all-done.6 = bf16[8,128,256]{2,1,0:T(8,128)(2,1)} async-done(((bf16[8,128,256]{2,1,0:T(8,128)(2,1)}), bf16[8,128,256]{2,1,0:T(8,128)(2,1)}, u32[]{:S(2)}, u32[]{:S(2)}) %all-to-all-start.6) | async-done | bytes 524320 | tf_op jit(solution)/shard_map/all_to_all | solution.py:178
  662.1 4.2 all-to-all-start.5
  675.5 16.4 %all-to-all-done.5 = bf16[8,128,512]{2,1,0:T(8,128)(2,1)} async-done(((bf16[8,128,512]{2,1,0:T(8,128)(2,1)}), bf16[8,128,512]{2,1,0:T(8,128)(2,1)}, u32[]{:S(2)}, u32[]{:S(2)}) %all-to-all-start.5) | async-done | bytes 1048608 | tf_op jit(solution)/shard_map/all_to_all | solution.py:175
  691.8 2.3 copy.65
  (128 shorter events, 50.7 us)
Async XLA Ops:
  7.2 307.7 %copy-start = (bf16[1,2048,768]{2,1,0:T(8,128)(2,1)S(1)}, bf16[1,2048,768]{2,1,0:T(8,128)(2,1)}, u32[]{:S(2)}) copy-start(bf16[1,2048,768]{2,1,0:T(8,128)(2,1)} %param.32) | copy-start | bytes 9437188
  64.9 237.3 %copy-start.20 = (bf16[1,768,2048]{2,1,0:T(8,128)(2,1)S(1)}, bf16[1,768,2048]{2,1,0:T(8,128)(2,1)}, u32[]{:S(2)}) copy-start(bf16[1,768,2048]{2,1,0:T(8,128)(2,1)} %param.33) | copy-start | bytes 9437188
  302.2 6.3 copy-start.3
  302.2 6.3 copy-start.21
  343.0 121.1 %all-to-all-start.1 = ((bf16[32,40,2048]{2,1,0:T(8,128)(2,1)}), bf16[32,40,2048]{2,1,0:T(8,128)(2,1)}, u32[]{:S(2)}, u32[]{:S(2)}) async-start(bf16[32,40,2048]{2,1,0:T(8,128)(2,1)} %add_convert_fusion), calls=%async_computation.1 | async-start | bytes 10485760 | tf_op jit(solution)/shard_map/all_to_all | solution.py:96
  346.6 269.4 %all-gather.2.cloned.1.call-start = ((), (), s32[]{:S(2)}) async-start(), calls=%async_computation.7 | async-start | bytes 4718592 | tf_op jit(solution)/shard_map/all_gather | solution.py:134
  476.1 5.2 copy-start.4
  476.1 5.2 copy-start.18
  476.1 5.4 copy-start.7
  476.1 6.7 copy-start.13
  482.8 5.6 copy-start.14
  483.5 51.2 %copy-start.16 = (bf16[128,512]{1,0:T(8,128)(2,1)S(1)}, bf16[128,512]{1,0:T(8,128)(2,1)}, u32[]{:S(2)}) copy-start(bf16[128,512]{1,0:T(8,128)(2,1)} %param.36) | copy-start | bytes 393220
  483.5 51.3 %copy-start.17 = (bf16[128,512]{1,0:T(8,128)(2,1)S(1)}, bf16[128,512]{1,0:T(8,128)(2,1)}, u32[]{:S(2)}) copy-start(bf16[128,512]{1,0:T(8,128)(2,1)} %param.37) | copy-start | bytes 393220
  484.8 46.3 %all-to-all-start.4 = ((bf16[128,8,512]{2,0,1:T(8,128)(2,1)}), bf16[128,8,512]{2,0,1:T(8,128)(2,1)S(1)}, u32[]{:S(2)}, u32[]{:S(2)}) async-start(bf16[128,8,512]{2,0,1:T(8,128)(2,1)} %copy.61), calls=%async_computation.4 | async-start | bytes 2097152 | tf_op jit(solution)/shard_map/all_to_all | solution.py:130
  488.4 104.2 %copy-start.19 = (f32[4,1024]{1,0:T(4,128)S(1)}, f32[4,1024]{1,0:T(4,128)}, u32[]{:S(2)}) copy-start(f32[4,1024]{1,0:T(4,128)} %param.39) | copy-start | bytes 49156
  531.1 57.1 %all-to-all-start.3 = ((bf16[128,8,512]{2,0,1:T(8,128)(2,1)}), bf16[128,8,512]{2,0,1:T(8,128)(2,1)S(1)}, u32[]{:S(2)}, u32[]{:S(2)}) async-start(bf16[128,8,512]{2,0,1:T(8,128)(2,1)} %bitcast.177), calls=%async_computation.3 | async-start | bytes 2097152 | tf_op jit(solution)/shard_map/all_to_all | solution.py:129
  588.2 5.0 copy-start.5
  588.2 18.4 %all-to-all-start.2 = ((bf16[128,8,256]{2,0,1:T(8,128)(2,1)}), bf16[128,8,256]{2,0,1:T(8,128)(2,1)}, u32[]{:S(2)}, u32[]{:S(2)}) async-start(bf16[128,8,256]{2,0,1:T(8,128)(2,1)} %all_to_all.66), calls=%async_computation.2 | async-start | bytes 1048576 | tf_op jit(solution)/shard_map/all_to_all | solution.py:131
  597.0 13.5 %copy-start.11 = (bf16[2048,128]{1,0:T(8,128)(2,1)}, bf16[2048,128]{1,0:T(8,128)(2,1)S(1)}, u32[]{:S(2)}) copy-start(bf16[2048,128]{1,0:T(8,128)(2,1)S(1)} %reshape.320) | copy-start | bytes 1572868
  598.5 17.5 %copy-start.8 = (bf16[2048,128]{1,0:T(8,128)(2,1)}, bf16[2048,128]{1,0:T(8,128)(2,1)S(1)}, u32[]{:S(2)}) copy-start(bf16[2048,128]{1,0:T(8,128)(2,1)S(1)} %reshape.323) | copy-start | bytes 1572868
  622.5 3.5 copy-start.2
  625.9 1.7 copy-start.12
  627.6 3.6 copy-start.6
  631.3 8.1 %slice-start = ((s8[8388608]{0:T(1024)(128)(4,1)}), s8[4194304]{0:T(1024)(128)(4,1)S(1)}, s32[]{:S(2)}) async-start(s8[8388608]{0:T(1024)(128)(4,1)} %bitcast.179), calls=%async_computation.8 | async-start | bytes 8388608
  632.8 6.6 slice-start.1
  632.8 6.6 copy-start.10
  639.4 2.3 copy-start.22
  639.4 2.3 copy-start.9
  639.4 2.3 copy-start.15
  643.9 18.3 %all-to-all-start.6 = ((bf16[8,128,256]{2,1,0:T(8,128)(2,1)}), bf16[8,128,256]{2,1,0:T(8,128)(2,1)}, u32[]{:S(2)}, u32[]{:S(2)}) async-start(bf16[8,128,256]{2,1,0:T(8,128)(2,1)} %pad_maximum_fusion.2), calls=%async_computation.6 | async-start | bytes 1048576 | tf_op jit(solution)/shard_map/all_to_all | solution.py:178
  662.1 29.7 %all-to-all-start.5 = ((bf16[8,128,512]{2,1,0:T(8,128)(2,1)}), bf16[8,128,512]{2,1,0:T(8,128)(2,1)}, u32[]{:S(2)}, u32[]{:S(2)}) async-start(bf16[8,128,512]{2,1,0:T(8,128)(2,1)} %bitcast.41), calls=%async_computation.5 | async-start | bytes 2097152 | tf_op jit(solution)/shard_map/all_to_all | solution.py:175
  666.4 30.0 %copy-start.1 = (bf16[1,2048,768]{2,1,0:T(8,128)(2,1)S(1)}, bf16[1,2048,768]{2,1,0:T(8,128)(2,1)}, u32[]{:S(2)}) copy-start(bf16[1,2048,768]{2,1,0:T(8,128)(2,1)} %param.32) | copy-start | bytes 9437188
Sparse Core Ops, SparseCore 0:
  482.9 109.5 all-gather.1
where the time goes:
time: 710 us; the launch traced here: 704 us
  waiting for transfers between devices  242 us (34%)
  blocking collectives  237 us (33%)
  matrix products  76.8 us (11%)
  local copies, waits for them, and re-layouts  73.8 us (10%)
  other arithmetic  34.9 us (5%)
  starting transfers between devices  23.5 us (3%)
  between operations  15.1 us (2%)
    all_to_all x1, blocking collectives, per_device(): lax.all_to_all(outgoing, ('grp', 'inner'), split_axis=0, concat_axis=0, t...  237 us
    all_to_all x1, waiting for transfers between devices, per_device(): lax.all_to_all(expert_grads(lax.all_to_all(outgoing, ('grp', 'inner'), sp...  117 us
    all_to_all x1, waiting for transfers between devices, per_device(): lax.all_to_all(queries, 'inner', split_axis=1, concat_axis=0, tiled=True)  51.5 us
    all_to_all x1, waiting for transfers between devices, per_device(): lax.all_to_all(attn_out, 'inner', split_axis=1, concat_axis=0, tiled=True)  41.6 us
    dot_general x5, matrix products, contract_last(): lax.dot_general(left, right, (((1,), (1,)), ((), ())), preferred_element_...  22.9 us
    dot_general x1, matrix products, expert_grads(): jnp.einsum('nlcf,ldf->nlcd', grad_gate, w_gate, preferred_element_type=jn...  16.7 us
    all_to_all x1, waiting for transfers between devices, per_device(): lax.all_to_all(grad_query_heads.astype(jnp.bfloat16), 'inner', split_axis...  16.4 us
  transfers between devices with their start and end apart: 7, of which 6 were waited for; matrix products, arithmetic and copies ran while one was open for 5% of the time, Pallas kernels for 0%

commit v1 on v0

--- a/solution.py
+++ b/solution.py
@@ -1,6 +1,10 @@
+import functools
+
 import jax
 import jax.numpy as jnp
 from jax import lax
+from jax.experimental import pallas as pl
+from jax.experimental.pallas import tpu as pltpu
 from jax.sharding import PartitionSpec as P
 
 KEY_VALUE_HEADS = 4
@@ -20,6 +24,19 @@
     return lax.dot_general(
         left, right, (((0,), (0,)), ((), ())), preferred_element_type=jnp.float32
     )
+
+
+def expert_rows_grads(inputs, upstream, gate_matrix, up_matrix, down_matrix):
+    gate_pre = jnp.dot(inputs, gate_matrix, preferred_element_type=jnp.float32)
+    up_pre = jnp.dot(inputs, up_matrix, preferred_element_type=jnp.float32)
+    back_hidden = contract_last(upstream, down_matrix)
+    sigmoid = jax.nn.sigmoid(gate_pre)
+    grad_gate = (back_hidden * up_pre * sigmoid * (1.0 + gate_pre * (1.0 - sigmoid))).astype(
+        jnp.bfloat16
+    )
+    grad_up = (back_hidden * gate_pre * sigmoid).astype(jnp.bfloat16)
+    grad_in = contract_last(grad_gate, gate_matrix) + contract_last(grad_up, up_matrix)
+    return grad_in.astype(jnp.bfloat16)
 
 
 def expert_grads(received, w_gate, w_up, w_down):
@@ -41,6 +58,303 @@
         "nlcf,ldf->nlcd", grad_up, w_up, preferred_element_type=jnp.float32
     )
     return grad_in.astype(jnp.bfloat16).reshape(received.shape[:-1] + (width,))
+
+
+MESH_ID = pl.DeviceIdType.MESH
+GATHER_LIMIT = 48 * 2**20
+
+
+def spread_kernel(
+    cols,
+    lines,
+    first_ref,
+    second_ref,
+    query_ref,
+    output_ref,
+    key_ref,
+    value_ref,
+    first_all,
+    second_all,
+    head_query,
+    head_output,
+    head_key,
+    head_value,
+    own_buf,
+    head_buf,
+    kv_buf,
+    send_sem,
+    recv_sem,
+    own_sem,
+    head_send,
+    head_recv,
+    head_own,
+):
+    group = lax.axis_index("grp")
+    place = lax.axis_index("inner")
+    peers = cols * lines
+    row_y, core = group // 2, group % 2
+    line, col = place // cols, place % cols
+    other_y, other_x = 1 - row_y, 1 - col
+    core_peer = (row_y * 2 + 1 - core, place)
+    x_peer = (group, line * cols + other_x)
+    y_peer = (other_y * 2 + core, place)
+    arrays = ((first_ref, first_all), (second_ref, second_all))
+    tokens = first_ref.shape[0]
+    head_width = head_query.shape[1]
+    kv_width = head_key.shape[1]
+    share = peers // (key_ref.shape[1] // kv_width)
+
+    def block(y, z, x, c=None):
+        return ((y * 2 + (core if c is None else c)) * peers) + z * cols + x
+
+    def inner_copies(to, slot, source, target):
+        columns = pl.ds(pl.multiple_of(to * head_width, head_width), head_width)
+        kv_columns = pl.ds(pl.multiple_of((to // share) * kv_width, kv_width), kv_width)
+        rows = pl.ds(pl.multiple_of(source * tokens, tokens), tokens)
+        pairs = (
+            (query_ref.at[:, columns], head_query.at[rows]),
+            (output_ref.at[:, columns], head_output.at[rows]),
+            (key_ref.at[:, kv_columns], head_key.at[rows]),
+            (value_ref.at[:, kv_columns], head_value.at[rows]),
+        )
+        return [
+            pltpu.make_async_remote_copy(
+                src_ref=src,
+                dst_ref=dst,
+                send_sem=head_send.at[number, slot],
+                recv_sem=head_recv.at[number, slot],
+                device_id=(group, target),
+                device_id_type=MESH_ID,
+            )
+            for number, (src, dst) in enumerate(pairs)
+        ]
+
+    barrier = pltpu.get_barrier_semaphore()
+    for step in range(1, peers):
+        pl.semaphore_signal(
+            barrier, inc=1, device_id=(group, lax.rem(place + step, peers)), device_id_type=MESH_ID
+        )
+    for peer in (core_peer, y_peer):
+        pl.semaphore_signal(barrier, inc=1, device_id=peer, device_id_type=MESH_ID)
+    pl.semaphore_wait(barrier, peers + 1)
+
+    def copy(which, index, way, peer, own):
+        source, gathered = arrays[which]
+        return pltpu.make_async_remote_copy(
+            src_ref=source if own else gathered.at[index],
+            dst_ref=gathered.at[index],
+            send_sem=send_sem.at[which, way, index],
+            recv_sem=recv_sem.at[which, index],
+            device_id=peer,
+            device_id_type=MESH_ID,
+        )
+
+    def arrived(which, index):
+        copy(which, index, 0, core_peer, False).wait_recv()
+
+    UP, DOWN, XWAY, YWAY, CORE = range(5)
+    sent = []
+
+    def send(which, index, way, peer, own=False):
+        copy(which, index, way, peer, own).start()
+
+    def z_peer(delta):
+        return (group, jnp.clip(line + delta, 0, lines - 1) * cols + col)
+
+    own_index = block(row_y, line, col)
+    local_in = [
+        pltpu.make_async_copy(arrays[w][0], own_buf.at[w], own_sem.at[w]) for w in range(2)
+    ]
+    own_columns = pl.ds(pl.multiple_of(place * head_width, head_width), head_width)
+    own_kv = pl.ds(pl.multiple_of((place // share) * kv_width, kv_width), kv_width)
+    own_rows = pl.ds(pl.multiple_of(place * tokens, tokens), tokens)
+    local_in += [
+        pltpu.make_async_copy(query_ref.at[:, own_columns], head_buf.at[0], head_own.at[0]),
+        pltpu.make_async_copy(output_ref.at[:, own_columns], head_buf.at[1], head_own.at[1]),
+        pltpu.make_async_copy(key_ref.at[:, own_kv], kv_buf.at[0], head_own.at[2]),
+        pltpu.make_async_copy(value_ref.at[:, own_kv], kv_buf.at[1], head_own.at[3]),
+    ]
+    local_out = [
+        pltpu.make_async_copy(own_buf.at[w], arrays[w][1].at[own_index], own_sem.at[2 + w])
+        for w in range(2)
+    ]
+    local_out += [
+        pltpu.make_async_copy(head_buf.at[0], head_query.at[own_rows], head_own.at[4]),
+        pltpu.make_async_copy(head_buf.at[1], head_output.at[own_rows], head_own.at[5]),
+        pltpu.make_async_copy(kv_buf.at[0], head_key.at[own_rows], head_own.at[6]),
+        pltpu.make_async_copy(kv_buf.at[1], head_value.at[own_rows], head_own.at[7]),
+    ]
+
+    def from_line(index, own, up, down):
+        if up is not None:
+            for w in range(2):
+
+                @pl.when(up)
+                def _():
+                    send(w, index, UP, z_peer(1), own)
+
+        if down is not None:
+            for w in range(2):
+
+                @pl.when(down)
+                def _():
+                    send(w, index, DOWN, z_peer(-1), own)
+
+        send(0, index, XWAY, x_peer, own)
+        send(1, index, YWAY, y_peer, own)
+        send(1, index, XWAY, x_peer, own)
+        send(0, index, YWAY, y_peer, own)
+        for w in range(2):
+            send(w, index, CORE, core_peer, own)
+
+    def from_plane(z):
+        index = block(row_y, z, other_x)
+        arrived(0, index)
+        send(0, index, YWAY, y_peer)
+        send(0, index, CORE, core_peer)
+        index = block(other_y, z, col)
+        arrived(1, index)
+        send(1, index, XWAY, x_peer)
+        send(1, index, CORE, core_peer)
+
+    def last_plane(z):
+        for w, index in (
+            (1, block(row_y, z, other_x)),
+            (0, block(other_y, z, col)),
+            (0, block(other_y, z, other_x)),
+            (1, block(other_y, z, other_x)),
+        ):
+            arrived(w, index)
+            send(w, index, CORE, core_peer)
+
+    def at_distance(distance, act):
+        for sign in (-1, 1):
+            z = line + sign * distance
+
+            @pl.when((z >= 0) & (z < lines))
+            def _():
+                act(z, sign)
+
+    from_line(own_index, True, line < lines - 1, line > 0)
+    for c in local_in:
+        c.start()
+
+    def head_start():
+        for step in range(1, peers):
+            to = lax.rem(place + step, peers)
+            for c in inner_copies(to, step, place, to):
+                c.start()
+
+    for distance in range(lines):
+        if distance:
+
+            def take(z, sign):
+                index = block(row_y, z, col)
+                for w in range(2):
+                    arrived(w, index)
+                up = (line < lines - 1) if sign < 0 else None
+                down = (line > 0) if sign > 0 else None
+                from_line(index, False, up, down)
+
+            at_distance(distance, take)
+        if distance == max(0, lines - 2):
+            head_start()
+        if distance == 0:
+            from_plane(line)
+            for c in local_in:
+                c.wait()
+            for c in local_out:
+                c.start()
+        else:
+            at_distance(distance, lambda z, sign: from_plane(z))
+
+    last_plane(line)
+    for distance in range(1, lines):
+        at_distance(distance, lambda z, sign: last_plane(z))
+
+    for y in range(2):
+        for z in range(lines):
+            for x in range(cols):
+                for w in range(2):
+                    arrived(w, block(y, z, x, 1 - core))
+    for step in range(1, peers):
+        source = lax.rem(place + peers - step, peers)
+        for c in inner_copies(place, step, source, source):
+            c.wait_recv()
+        for c in inner_copies(lax.rem(place + step, peers), step, place, source):
+            c.wait_send()
+    for c in local_out:
+        c.wait()
+
+    def sent_wait(which, index, way):
+        copy(which, index, way, core_peer, False).wait_send()
+
+    for z in range(lines):
+        index = block(row_y, z, col)
+        for w in range(2):
+            for way in (XWAY, YWAY):
+                sent_wait(w, index, way)
+
+            @pl.when((z <= line) & (line < lines - 1))
+            def _():
+                sent_wait(w, index, UP)
+
+            @pl.when((z >= line) & (line > 0))
+            def _():
+                sent_wait(w, index, DOWN)
+
+        sent_wait(0, block(row_y, z, other_x), YWAY)
+        sent_wait(1, block(other_y, z, col), XWAY)
+        for y in range(2):
+            for x in range(cols):
+                for w in range(2):
+                    sent_wait(w, block(y, z, x), CORE)
+
+
+def spread(first, second, queries, attn_out, keys, values, devices, peers, cols):
+    tokens, width = first.shape
+    head_width = queries.shape[1] // peers
+    any_space = pl.BlockSpec(memory_space=pl.ANY)
+    kind = first.dtype
+    shapes = (
+        jax.ShapeDtypeStruct((devices, tokens, width), kind),
+        jax.ShapeDtypeStruct((devices, tokens, width), kind),
+        jax.ShapeDtypeStruct((peers * tokens, head_width), kind),
+        jax.ShapeDtypeStruct((peers * tokens, head_width), kind),
+        jax.ShapeDtypeStruct((peers * tokens, HEAD_SIZE), kind),
+        jax.ShapeDtypeStruct((peers * tokens, HEAD_SIZE), kind),
+    )
+    return pl.pallas_call(
+        functools.partial(spread_kernel, cols, peers // cols),
+        out_shape=shapes,
+        in_specs=[any_space] * 6,
+        out_specs=[any_space] * 6,
+        scratch_shapes=[
+            pltpu.VMEM((2, tokens, width), kind),
+            pltpu.VMEM((2, tokens, head_width), kind),
+            pltpu.VMEM((2, tokens, HEAD_SIZE), kind),
+            pltpu.SemaphoreType.DMA((2, 5, devices)),
+            pltpu.SemaphoreType.DMA((2, devices)),
+            pltpu.SemaphoreType.DMA((4,)),
+            pltpu.SemaphoreType.DMA((4, peers)),
+            pltpu.SemaphoreType.DMA((4, peers)),
+            pltpu.SemaphoreType.DMA((8,)),
+        ],
+        compiler_params=pltpu.CompilerParams(
+            collective_id=0, has_side_effects=True, vmem_limit_bytes=8 * 2**20
+        ),
+        cost_estimate=pl.CostEstimate(
+            flops=0, bytes_accessed=500 * 2**20, transcendentals=0
+        ),
+    )(first, second, queries, attn_out, keys, values)
+
+
+def slot_ranks(named):
+    tokens = named.shape[1]
+    before = jnp.triu(jnp.ones((tokens, tokens), jnp.bfloat16), 1)
+    return jnp.dot(named.astype(jnp.bfloat16), before, preferred_element_type=jnp.float32).astype(
+        jnp.int32
+    )
 
 
 def per_device(
@@ -69,44 +383,99 @@
     inverse = lax.rsqrt(jnp.mean(hidden_f * hidden_f, axis=1, keepdims=True) + EPSILON)
     normed = (hidden_f * inverse * norm_gain).astype(jnp.bfloat16)
     upstream = grad_out.astype(jnp.float32)
-    flat_count = token_rows * topk
-    flat_ids = expert_ids.reshape(-1)
-    one_hot = (flat_ids[:, None] == jnp.arange(experts_all, dtype=jnp.int32)[None, :]).astype(
-        jnp.int32
-    )
-    slot_rank = jnp.sum((jnp.cumsum(one_hot, axis=0) - one_hot) * one_hot, axis=1)
-    target = flat_ids * capacity + slot_rank
-    owner = (
-        jnp.full((experts_all * capacity,), flat_count, jnp.int32)
-        .at[target]
-        .set(jnp.arange(flat_count, dtype=jnp.int32))
-    )
-    source_tok = owner // topk
-    scaled = (
-        (upstream[:, None, :] * gate_weights[:, :, None])
-        .reshape(flat_count, width)
-        .astype(jnp.bfloat16)
-    )
-    zero_row = jnp.zeros((1, width), jnp.bfloat16)
-    slot_inputs = jnp.concatenate([normed, zero_row], axis=0)[source_tok]
-    slot_grads = jnp.concatenate([scaled, zero_row], axis=0)[owner]
-    outgoing = jnp.concatenate([slot_inputs, slot_grads], axis=1).reshape(
-        experts_all, capacity, 2 * width
-    )
-    returned = lax.all_to_all(
-        expert_grads(
-            lax.all_to_all(outgoing, ("grp", "inner"), split_axis=0, concat_axis=0, tiled=True),
-            w_gate,
-            w_up,
-            w_down,
-        ),
-        ("grp", "inner"),
-        split_axis=0,
-        concat_axis=0,
-        tiled=True,
-    )
-    expert_rows = returned.reshape(-1, width)[target].astype(jnp.float32)
-    grad_normed = jnp.sum(expert_rows.reshape(token_rows, topk, width), axis=1)
+    cols = groups // 2
+    devices = groups * inner_product
+    gather_plan = (
+        cols == 2
+        and inner_product % cols == 0
+        and w_gate.shape[0] == 1
+        and 2 * devices * hidden.size * hidden.dtype.itemsize <= GATHER_LIMIT
+    )
+    if gather_plan:
+        meta = jnp.concatenate(
+            [expert_ids.astype(jnp.float32).T, gate_weights.T], axis=0
+        )
+        meta_all = lax.all_gather(meta, ("grp", "inner"), axis=0, tiled=True).reshape(
+            devices, 2, topk, token_rows
+        )
+        normed_all, upstream_all, head_query, head_output, head_key, head_value = spread(
+            normed, grad_out, queries, attn_out, keys, values, devices, inner_product, cols
+        )
+        expert = lax.axis_index("grp") * inner_product + lax.axis_index("inner")
+        chosen = meta_all[:, 0].astype(jnp.int32) == expert
+        named = jnp.any(chosen, axis=1)
+        weight = jnp.sum(jnp.where(chosen, meta_all[:, 1], 0.0), axis=1)
+        pick = (
+            jnp.arange(capacity, dtype=jnp.int32)[None, :, None] == slot_ranks(named)[:, None, :]
+        ) & named[:, None, :]
+        slot_weight = jnp.sum(jnp.where(pick, weight[:, None, :], 0.0), axis=2)
+        pick = pick.astype(jnp.bfloat16)
+        slot_inputs = jnp.einsum("dct,dtw->dcw", pick, normed_all)
+        slot_grads = jnp.einsum(
+            "dct,dtw->dcw", pick, upstream_all, preferred_element_type=jnp.float32
+        )
+        slot_grads = (slot_grads * slot_weight[:, :, None]).astype(jnp.bfloat16)
+        returned = lax.all_to_all(
+            expert_rows_grads(
+                slot_inputs.reshape(-1, width), slot_grads.reshape(-1, width), w_gate[0], w_up[0], w_down[0]
+            ),
+            ("grp", "inner"),
+            split_axis=0,
+            concat_axis=0,
+            tiled=True,
+        )
+        mine = jnp.any(
+            expert_ids.T[None] == jnp.arange(experts_all, dtype=jnp.int32)[:, None, None], axis=1
+        )
+        place = (
+            (
+                jnp.arange(capacity, dtype=jnp.int32)[None, :, None]
+                == slot_ranks(mine)[:, None, :]
+            )
+            & mine[:, None, :]
+        ).astype(jnp.bfloat16)
+        grad_normed = contract_first(
+            place.reshape(experts_all * capacity, token_rows), returned
+        )
+    else:
+        flat_count = token_rows * topk
+        flat_ids = expert_ids.reshape(-1)
+        one_hot = (flat_ids[:, None] == jnp.arange(experts_all, dtype=jnp.int32)[None, :]).astype(
+            jnp.int32
+        )
+        slot_rank = jnp.sum((jnp.cumsum(one_hot, axis=0) - one_hot) * one_hot, axis=1)
+        target = flat_ids * capacity + slot_rank
+        owner = (
+            jnp.full((experts_all * capacity,), flat_count, jnp.int32)
+            .at[target]
+            .set(jnp.arange(flat_count, dtype=jnp.int32))
+        )
+        source_tok = owner // topk
+        scaled = (
+            (upstream[:, None, :] * gate_weights[:, :, None])
+            .reshape(flat_count, width)
+            .astype(jnp.bfloat16)
+        )
+        zero_row = jnp.zeros((1, width), jnp.bfloat16)
+        slot_inputs = jnp.concatenate([normed, zero_row], axis=0)[source_tok]
+        slot_grads = jnp.concatenate([scaled, zero_row], axis=0)[owner]
+        outgoing = jnp.concatenate([slot_inputs, slot_grads], axis=1).reshape(
+            experts_all, capacity, 2 * width
+        )
+        returned = lax.all_to_all(
+            expert_grads(
+                lax.all_to_all(outgoing, ("grp", "inner"), split_axis=0, concat_axis=0, tiled=True),
+                w_gate,
+                w_up,
+                w_down,
+            ),
+            ("grp", "inner"),
+            split_axis=0,
+            concat_axis=0,
+            tiled=True,
+        )
+        expert_rows = returned.reshape(-1, width)[target].astype(jnp.float32)
+        grad_normed = jnp.sum(expert_rows.reshape(token_rows, topk, width), axis=1)
     gained = grad_normed * norm_gain
     statistic = jnp.mean(gained * hidden_f, axis=1, keepdims=True)
     grad_resid = (
@@ -115,27 +484,29 @@
     head_width = queries.shape[1] // inner_product
     per_head = head_width // HEAD_SIZE
     shared_portion = inner_product // KEY_VALUE_HEADS
-    key_value_pairs = jnp.concatenate(
-        [
-            keys.reshape(token_rows, KEY_VALUE_HEADS, 1, HEAD_SIZE),
-            values.reshape(token_rows, KEY_VALUE_HEADS, 1, HEAD_SIZE),
-        ],
-        axis=2,
-    )
-    key_value_broadcast = jnp.broadcast_to(
-        key_value_pairs[:, :, None], (token_rows, KEY_VALUE_HEADS, shared_portion, 2, HEAD_SIZE)
-    ).reshape(token_rows, inner_product * 2 * HEAD_SIZE)
-    head_query, head_output, head_kv = (
-        lax.all_to_all(queries, "inner", split_axis=1, concat_axis=0, tiled=True),
-        lax.all_to_all(attn_out, "inner", split_axis=1, concat_axis=0, tiled=True),
-        lax.all_to_all(key_value_broadcast, "inner", split_axis=1, concat_axis=0, tiled=True),
-    )
+    if not gather_plan:
+        key_value_pairs = jnp.concatenate(
+            [
+                keys.reshape(token_rows, KEY_VALUE_HEADS, 1, HEAD_SIZE),
+                values.reshape(token_rows, KEY_VALUE_HEADS, 1, HEAD_SIZE),
+            ],
+            axis=2,
+        )
+        key_value_broadcast = jnp.broadcast_to(
+            key_value_pairs[:, :, None], (token_rows, KEY_VALUE_HEADS, shared_portion, 2, HEAD_SIZE)
+        ).reshape(token_rows, inner_product * 2 * HEAD_SIZE)
+        head_query, head_output, head_kv = (
+            lax.all_to_all(queries, "inner", split_axis=1, concat_axis=0, tiled=True),
+            lax.all_to_all(attn_out, "inner", split_axis=1, concat_axis=0, tiled=True),
+            lax.all_to_all(key_value_broadcast, "inner", split_axis=1, concat_axis=0, tiled=True),
+        )
     head_grad = contract_last(
         lax.all_gather(grad_resid, "inner", axis=0, tiled=True), w_out
     ).astype(jnp.bfloat16)
     seq_len = head_query.shape[0]
-    head_key = head_kv[:, :HEAD_SIZE]
-    head_value = head_kv[:, HEAD_SIZE:]
+    if not gather_plan:
+        head_key = head_kv[:, :HEAD_SIZE]
+        head_value = head_kv[:, HEAD_SIZE:]
     lse_rows = lse.T
     scale = float(HEAD_SIZE) ** (-0.5)
     blocks = 1

time: 710 us -> 614 us (0.86)
  Pallas kernels: 0 us -> 168 us
  blocking collectives: 237 us -> 71.2 us
  waiting for transfers between devices: 242 us -> 195 us
  local copies, waits for them, and re-layouts: 73.8 us -> 41.1 us
  other arithmetic: 34.9 us -> 13.3 us
  starting transfers between devices: 23.5 us -> 12.8 us
  matrix products: 76.8 us -> 86.6 us
    all_to_all x1 -> x0, blocking collectives: 237 us -> none  [per_device(): lax.all_to_all(outgoing, ('grp', 'inner'), split_axis=0, concat_axis=0, t...]
    pallas_call x0 -> x1, Pallas kernels: none -> 168 us  [spread(): pl.pallas_call(functools.partial(spread_kernel, cols, peers // cols), out...]
    all_to_all x4 -> x1, waiting for transfers between devices: 219 us -> 117 us  [per_device(): lax.all_to_all(expert_rows_grads(slot_inputs.reshape(-1, width), slot_gra...]
    all_gather x0 -> x1, blocking collectives: none -> 71.2 us  [per_device(): lax.all_gather(meta, ('grp', 'inner'), axis=0, tiled=True)]
    all_gather x1, waiting for transfers between devices: 0.01 us -> 54.2 us  [per_device(): lax.all_gather(grad_resid, 'inner', axis=0, tiled=True)]
    gather x3 -> x0, local copies, waits for them, and re-layouts: 37.5 us -> none  [the longest x1 13.6 us: per_device(): slot_grads = jnp.concatenate([scaled, zero_row], axis=0)[owner]]
    dot_general x5 -> x8, matrix products: 22.9 us -> 42.2 us  [contract_last(): lax.dot_general(left, right, (((1,), (1,)), ((), ())), preferred_element_...]
    unnamed x56 -> x71, local copies, waits for them, and re-layouts: 6.32 us -> 23.7 us
  transfers between devices with their start and end apart: 7 -> 4, of which waited for: 6 -> 4; matrix products, arithmetic and copies ran while one was open for 5% -> 5% of each run, Pallas kernels for 0% -> 0%
where the time goes in v1:
time: 614 us; the launch traced here: 603 us
  waiting for transfers between devices  195 us (32%)
  Pallas kernels  168 us (27%)
  matrix products  86.6 us (14%)
  blocking collectives  71.2 us (12%)
  local copies, waits for them, and re-layouts  41.1 us (7%)
  between operations  15 us (2%)
  other arithmetic  13.3 us (2%)
  starting transfers between devices  12.8 us (2%)
    pallas_call x1, Pallas kernels, spread(): pl.pallas_call(functools.partial(spread_kernel, cols, peers // cols), out...  168 us
    all_to_all x1, waiting for transfers between devices, per_device(): lax.all_to_all(expert_rows_grads(slot_inputs.reshape(-1, width), slot_gra...  117 us
    all_gather x1, blocking collectives, per_device(): lax.all_gather(meta, ('grp', 'inner'), axis=0, tiled=True)  71.2 us
    all_gather x1, waiting for transfers between devices, per_device(): lax.all_gather(grad_resid, 'inner', axis=0, tiled=True)  54.2 us
    dot_general x8, matrix products, contract_last(): lax.dot_general(left, right, (((1,), (1,)), ((), ())), preferred_element_...  42.2 us
    unnamed x71, local copies, waits for them, and re-layouts  23.7 us
    all_to_all x1, waiting for transfers between devices, per_device(): lax.all_to_all(grad_query_heads.astype(jnp.bfloat16), 'inner', split_axis...  15.8 us
    dot_general x5, matrix products, contract_first(): lax.dot_general(left, right, (((0,), (0,)), ((), ())), preferred_element_...  13.8 us
  transfers between devices with their start and end apart: 4, of which 4 were waited for; matrix products, arithmetic and copies ran while one was open for 5% of the time, Pallas kernels for 0%

profile of v1, /device:TPU:0, one launch (start us, length us, event | category | flops | bytes accessed | tf_op | source)
XLA Modules:
  0.0 603.2 jit_solution(13725728754790511484)
XLA Ops:
  8.8 71.2 %all_gather.6 = f32[512,128]{1,0:T(8,128)S(1)} all-gather(f32[16,128]{1,0:T(8,128)S(1)} %pad_maximum_fusion.2), channel_id=1, replica_groups=mesh['grp'=4,'inner'=8] {'grp','inner'}, dimensions={0}, use_global_device_ids=true | all-gather | bytes 270336 | tf_op jit(solution)/shard_map/all_gather | solution.py:398
  88.4 168.5 %shard_map.175 = (bf16[32,128,2048]{2,1,0:T(8,128)(2,1)S(1)}, bf16[32,128,2048]{2,1,0:T(8,128)(2,1)S(1)}, bf16[1024,512]{1,0:T(8,128)(2,1)S(1)}, bf16[1024,512]{...) custom-call(bf16[128,2048]{1,0:T(8,128)(2,1)S(1)} %fusion.30.first_ref, ...), custom_call_target="tpu_custom_call" | custom-call | bytes 524288000 | tf_op jit(solution)/shard_map/pallas_call | solution.py:327
  256.9 5.7 copy-done.2
  262.6 5.7 copy-done.3
  271.0 8.1 %fusion.40 = bf16[32,40,2048]{2,1,0:T(8,128)(2,1)S(1)} fusion(bf16[32,128,2048]{2,1,0:T(8,128)(2,1)} %copy-done.3, s32[32,128]{1,0:T(8,128)S(1)} %convolution_convert_fusion.1, pred[32,128]{1,0:T(8,128)(4,1)S(1)} %reduce_or.19), kind=kOutput, calls=%fused_computation.62 | convolution fusion | flops 671416320 | bytes 22040576 | tf_op jit(solution)/shard_map/dct,dtw->dcw/dot_general | solution.py:413
  279.1 8.2 %multiply_convert_fusion = bf16[32,40,2048]{2,1,0:T(8,128)(2,1)S(1)} fusion(f32[32,40]{1,0:T(8,128)S(1)} %select_reduce_fusion, bf16[32,128,2048]{2,1,0:T(8,128)(2,1)} %copy-done.2, s32[32,128]{1,0:T(8,128)S(1)} %convolution_convert_fusion.1, pred[32,128]{1,0:T(8,128)(4,1)S(1)} %reduce_or.19), kind=kOutput, calls=%fused_computation.1 | convolution fusion | flops 676659200 | bytes 22045696 | tf_op jit(solution)/shard_map/dct,dtw->dcw/dot_general | solution.py:414
  287.3 4.4 fusion.12
  291.7 4.5 fusion.8
  296.3 5.4 fusion.5
  301.7 6.9 %fusion.6 = f32[1280,2048]{1,0:T(8,128)} fusion(bf16[1280,768]{1,0:T(8,128)(2,1)S(1)} %fusion.5, bf16[1,2048,768]{2,1,0:T(8,128)(2,1)S(1)} %copy-done), kind=kOutput, calls=%fused_computation.16 | convolution fusion | flops 4026531840 | bytes 15597568 | tf_op jit(solution)/shard_map/dot_general | solution.py:18
  308.6 10.1 %add_convert_fusion = bf16[1280,2048]{1,0:T(8,128)(2,1)} fusion(f32[1280,2048]{1,0:T(8,128)} %fusion.6, bf16[1,2048,768]{2,1,0:T(8,128)(2,1)S(1)} %copy-done.27, f32[1280,768]{1,0:T(8,128)S(1)} %copy-done.30, f32[1280,768]{1,0:T(8,128)} %copy-done.31), kind=kOutput, calls=%fused_computation | convolution fusion | flops 4037672960 | bytes 26738688 | tf_op jit(solution)/shard_map/dot_general | solution.py:18
  318.7 4.1 all-to-all-start
  323.4 117.0 %all-to-all-done = bf16[32,40,2048]{2,1,0:T(8,128)(2,1)} async-done(((bf16[32,40,2048]{2,1,0:T(8,128)(2,1)}), bf16[32,40,2048]{2,1,0:T(8,128)(2,1)}, u32[]{:S(2)}, u32[]{:S(2)}) %all-to-all-start) | async-done | bytes 5242912 | tf_op jit(solution)/shard_map/all_to_all | solution.py:418
  440.4 3.5 fusion.36
  448.0 2.2 reshape.211
  453.2 4.1 exponential_select_fusion.1
  457.3 4.5 fusion.77
  461.8 54.2 %all-gather.2.cloned.1.call-done = bf16[1024,2048]{1,0:T(8,128)(2,1)} async-done(((bf16[128,2048]{1,0:T(8,128)(2,1)}), bf16[1024,2048]{1,0:T(8,128)(2,1)}) %all-gather.2.cloned.1.call-update) | async-done | bytes 4194320 | tf_op jit(solution)/shard_map/all_gather | solution.py:504
  516.0 5.2 convolution_convert_fusion
  522.9 3.1 fusion.17
  529.9 1.8 multiply_reduce_fusion
  531.7 6.2 %multiply_convert_fusion.1 = bf16[2048,1024]{1,0:T(8,128)(2,1)S(1)} fusion(f32[2048,1024]{1,0:T(8,128)} %fusion.77, bf16[2048,128]{1,0:T(8,128)(2,1)S(1)} %reshape.215, bf16[1024,128]{1,0:T(8,128)(2,1)S(1)} %copy-done.15, f32[2048]{0:T(1024)S(1)} %multiply_reduce_fusion, f32[2048]{0:T(1024)S(1)} %sub.60, s32[2048]{0:T(1024)S(1)} %broadcast_add_fusion), kind=kOutput, calls=%fused_computation.2 | convolution fusion | flops 551550976 | bytes 13393920 | tf_op jit(solution)/shard_map/dot_general | solution.py:18
  538.0 4.5 fusion.26
  544.6 4.1 all-to-all-start.2
  549.8 3.4 fusion.16
  554.6 7.7 %all-to-all-done.2 = bf16[8,128,256]{2,1,0:T(8,128)(2,1)} async-done(((bf16[8,128,256]{2,1,0:T(8,128)(2,1)}), bf16[8,128,256]{2,1,0:T(8,128)(2,1)}, u32[]{:S(2)}, u32[]{:S(2)}) %all-to-all-start.2) | async-done | bytes 524320 | tf_op jit(solution)/shard_map/all_to_all | solution.py:549
  562.4 4.2 all-to-all-start.1
  566.6 2.1 convert_element_type.126
  568.7 2.0 reduce.12
  575.6 15.8 %all-to-all-done.1 = bf16[8,128,512]{2,1,0:T(8,128)(2,1)} async-done(((bf16[8,128,512]{2,1,0:T(8,128)(2,1)}), bf16[8,128,512]{2,1,0:T(8,128)(2,1)}, u32[]{:S(2)}, u32[]{:S(2)}) %all-to-all-start.1) | async-done | bytes 1048608 | tf_op jit(solution)/shard_map/all_to_all | solution.py:546
  591.4 2.3 copy.34
  593.7 2.3 copy.37
  (110 shorter events, 35.1 us)
Async XLA Ops:
  7.2 284.6 %copy-start = (bf16[1,2048,768]{2,1,0:T(8,128)(2,1)S(1)}, bf16[1,2048,768]{2,1,0:T(8,128)(2,1)}, u32[]{:S(2)}) copy-start(bf16[1,2048,768]{2,1,0:T(8,128)(2,1)} %param.31) | copy-start | bytes 9437188
  84.1 1.2 copy-start.10
  85.3 1.2 copy-start.11
  256.9 5.7 copy-start.2
  262.6 5.7 copy-start.3
  279.1 8.2 %copy-start.26 = (bf16[1,768,2048]{2,1,0:T(8,128)(2,1)S(1)}, bf16[1,768,2048]{2,1,0:T(8,128)(2,1)}, u32[]{:S(2)}) copy-start(bf16[1,768,2048]{2,1,0:T(8,128)(2,1)} %param.33) | copy-start | bytes 9437188
  291.7 4.6 copy-start.29
  291.7 4.5 copy-start.27
  296.3 5.4 copy-start.31
  301.7 6.9 %copy-start.30 = (f32[1280,768]{1,0:T(8,128)S(1)}, f32[1280,768]{1,0:T(8,128)}, u32[]{:S(2)}) copy-start(f32[1280,768]{1,0:T(8,128)} %copy-done.29) | copy-start | bytes 11796484
  318.7 4.4 copy-start.25
  318.7 121.7 %copy-start.17 = (bf16[128,2048]{1,0:T(8,128)(2,1)S(1)}, bf16[128,2048]{1,0:T(8,128)(2,1)}, u32[]{:S(2)}) copy-start(bf16[128,2048]{1,0:T(8,128)(2,1)} %param.27) | copy-start | bytes 1572868
  318.7 121.7 %copy-start.23 = (f32[2048]{0:T(1024)S(1)}, f32[2048]{0:T(1024)}, u32[]{:S(2)}) copy-start(f32[2048]{0:T(1024)} %param.28) | copy-start | bytes 24580
  318.7 121.7 %all-to-all-start = ((bf16[32,40,2048]{2,1,0:T(8,128)(2,1)}), bf16[32,40,2048]{2,1,0:T(8,128)(2,1)}, u32[]{:S(2)}, u32[]{:S(2)}) async-start(bf16[32,40,2048]{2,1,0:T(8,128)(2,1)} %bitcast.68), calls=%async_computation | async-start | bytes 10485760 | tf_op jit(solution)/shard_map/all_to_all | solution.py:418
  322.9 121.0 %copy-start.5 = (bf16[128,2048]{1,0:T(8,128)(2,1)S(1)}, bf16[128,2048]{1,0:T(8,128)(2,1)}, u32[]{:S(2)}) copy-start(bf16[128,2048]{1,0:T(8,128)(2,1)} %second_ref.1) | copy-start | bytes 1572868
  322.9 193.1 %all-gather.2.cloned.1.call-start = ((), (), s32[]{:S(2)}) async-start(), calls=%async_computation.3 | async-start | bytes 4718592 | tf_op jit(solution)/shard_map/all_gather | solution.py:504
  323.3 121.8 %copy-start.7 = (bf16[1024,512]{1,0:T(8,128)(2,1)S(1)}, bf16[1024,512]{1,0:T(8,128)(2,1)}, u32[]{:S(2)}) copy-start(bf16[1024,512]{1,0:T(8,128)(2,1)} %copy-done.6) | copy-start | bytes 3145732
  323.3 121.8 %copy-start.9 = (bf16[1024,512]{1,0:T(8,128)(2,1)S(1)}, bf16[1024,512]{1,0:T(8,128)(2,1)}, u32[]{:S(2)}) copy-start(bf16[1024,512]{1,0:T(8,128)(2,1)} %copy-done.8) | copy-start | bytes 3145732
  445.2 5.0 copy-start.24
  452.9 9.0 %copy-start.18 = (bf16[2048,128]{1,0:T(8,128)(2,1)}, bf16[2048,128]{1,0:T(8,128)(2,1)S(1)}, u32[]{:S(2)}) copy-start(bf16[2048,128]{1,0:T(8,128)(2,1)S(1)} %reshape.214) | copy-start | bytes 1572868
  522.5 3.5 copy-start.15
  522.5 3.5 copy-start.16
  526.0 1.1 copy-start.21
  529.9 1.8 copy-start.20
  529.9 8.0 %slice-start = ((s8[8388608]{0:T(1024)(128)(4,1)}), s8[4194304]{0:T(1024)(128)(4,1)S(1)}, s32[]{:S(2)}) async-start(s8[8388608]{0:T(1024)(128)(4,1)} %bitcast.63), calls=%async_computation.4 | async-start | bytes 8388608
  531.7 6.2 %slice-start.1 = ((s8[8388608]{0:T(1024)(128)(4,1)}), s8[4194304]{0:T(1024)(128)(4,1)S(1)}, s32[]{:S(2)}) async-start(s8[8388608]{0:T(1024)(128)(4,1)} %bitcast.63), calls=%async_computation.5 | async-start | bytes 8388608
  537.9 4.5 copy-start.28
  538.0 4.5 copy-start.19
  538.0 4.5 copy-start.22
  544.6 17.7 %all-to-all-start.2 = ((bf16[8,128,256]{2,1,0:T(8,128)(2,1)}), bf16[8,128,256]{2,1,0:T(8,128)(2,1)}, u32[]{:S(2)}, u32[]{:S(2)}) async-start(bf16[8,128,256]{2,1,0:T(8,128)(2,1)} %pad_maximum_fusion.1), calls=%async_computation.2 | async-start | bytes 1048576 | tf_op jit(solution)/shard_map/all_to_all | solution.py:549
  562.4 29.0 %all-to-all-start.1 = ((bf16[8,128,512]{2,1,0:T(8,128)(2,1)}), bf16[8,128,512]{2,1,0:T(8,128)(2,1)}, u32[]{:S(2)}, u32[]{:S(2)}) async-start(bf16[8,128,512]{2,1,0:T(8,128)(2,1)} %bitcast.12), calls=%async_computation.1 | async-start | bytes 2097152 | tf_op jit(solution)/shard_map/all_to_all | solution.py:546
  566.6 29.3 %copy-start.1 = (bf16[1,2048,768]{2,1,0:T(8,128)(2,1)S(1)}, bf16[1,2048,768]{2,1,0:T(8,128)(2,1)}, u32[]{:S(2)}) copy-start(bf16[1,2048,768]{2,1,0:T(8,128)(2,1)} %param.31) | copy-start | bytes 9437188
  (6 other events, 5.5 us)
Sparse Core Ops, SparseCore 0:
  445.3 70.7 all-gather.1

commit v2 on v1

--- a/solution.py
+++ b/solution.py
@@ -79,7 +79,8 @@
     head_output,
     head_key,
     head_value,
-    own_buf,
+    own_first,
+    own_second,
     head_buf,
     kv_buf,
     send_sem,
@@ -99,6 +100,7 @@
     x_peer = (group, line * cols + other_x)
     y_peer = (other_y * 2 + core, place)
     arrays = ((first_ref, first_all), (second_ref, second_all))
+    own_bufs = (own_first, own_second)
     tokens = first_ref.shape[0]
     head_width = head_query.shape[1]
     kv_width = head_key.shape[1]
@@ -163,7 +165,7 @@
 
     own_index = block(row_y, line, col)
     local_in = [
-        pltpu.make_async_copy(arrays[w][0], own_buf.at[w], own_sem.at[w]) for w in range(2)
+        pltpu.make_async_copy(arrays[w][0], own_bufs[w], own_sem.at[w]) for w in range(2)
     ]
     own_columns = pl.ds(pl.multiple_of(place * head_width, head_width), head_width)
     own_kv = pl.ds(pl.multiple_of((place // share) * kv_width, kv_width), kv_width)
@@ -175,7 +177,7 @@
         pltpu.make_async_copy(value_ref.at[:, own_kv], kv_buf.at[1], head_own.at[3]),
     ]
     local_out = [
-        pltpu.make_async_copy(own_buf.at[w], arrays[w][1].at[own_index], own_sem.at[2 + w])
+        pltpu.make_async_copy(own_bufs[w], arrays[w][1].at[own_index], own_sem.at[2 + w])
         for w in range(2)
     ]
     local_out += [
@@ -312,13 +314,13 @@
 
 
 def spread(first, second, queries, attn_out, keys, values, devices, peers, cols):
-    tokens, width = first.shape
+    tokens = first.shape[0]
     head_width = queries.shape[1] // peers
     any_space = pl.BlockSpec(memory_space=pl.ANY)
     kind = first.dtype
     shapes = (
-        jax.ShapeDtypeStruct((devices, tokens, width), kind),
-        jax.ShapeDtypeStruct((devices, tokens, width), kind),
+        jax.ShapeDtypeStruct((devices,) + first.shape, kind),
+        jax.ShapeDtypeStruct((devices,) + second.shape, kind),
         jax.ShapeDtypeStruct((peers * tokens, head_width), kind),
         jax.ShapeDtypeStruct((peers * tokens, head_width), kind),
         jax.ShapeDtypeStruct((peers * tokens, HEAD_SIZE), kind),
@@ -330,7 +332,8 @@
         in_specs=[any_space] * 6,
         out_specs=[any_space] * 6,
         scratch_shapes=[
-            pltpu.VMEM((2, tokens, width), kind),
+            pltpu.VMEM(first.shape, kind),
+            pltpu.VMEM(second.shape, kind),
             pltpu.VMEM((2, tokens, head_width), kind),
             pltpu.VMEM((2, tokens, HEAD_SIZE), kind),
             pltpu.SemaphoreType.DMA((2, 5, devices)),
@@ -347,6 +350,67 @@
             flops=0, bytes_accessed=500 * 2**20, transcendentals=0
         ),
     )(first, second, queries, attn_out, keys, values)
+
+
+META_LANES = 128
+
+
+def pick_kernel(expert_ref, first_ref, second_ref, inputs_ref, grads_ref):
+    width = inputs_ref.shape[1]
+    capacity = inputs_ref.shape[0]
+    tokens, first_width = first_ref.shape
+    topk = expert_ref[1]
+    meta = first_ref[:, first_width - META_LANES :]
+    lane = lax.broadcasted_iota(jnp.int32, (tokens, META_LANES), 1)
+    chosen = jnp.where(
+        (meta.astype(jnp.float32) == expert_ref[0].astype(jnp.float32)) & (lane < topk), 1.0, 0.0
+    )
+    source = lax.broadcasted_iota(jnp.int32, (META_LANES, META_LANES), 0)
+    target = lax.broadcasted_iota(jnp.int32, (META_LANES, META_LANES), 1)
+    away = source - target
+    fold = (
+        (target < topk) & ((away == topk) | (away == 2 * topk) | (away == 3 * topk))
+    ).astype(jnp.float32).astype(jnp.bfloat16)
+    gates = jnp.dot(meta, fold, preferred_element_type=jnp.float32)
+    weight = jnp.sum(chosen * gates, axis=1, keepdims=True)
+    named = contract_last(jnp.ones((8, META_LANES), jnp.bfloat16), chosen.astype(jnp.bfloat16))
+    row = lax.broadcasted_iota(jnp.int32, (tokens, tokens), 0)
+    column = lax.broadcasted_iota(jnp.int32, (tokens, tokens), 1)
+    before = (row < column).astype(jnp.float32).astype(jnp.bfloat16)
+    rank = jnp.dot(named.astype(jnp.bfloat16), before, preferred_element_type=jnp.float32)
+    slot = lax.broadcasted_iota(jnp.int32, (capacity, tokens), 0).astype(jnp.float32)
+    pick = jnp.where((slot == rank[:1]) & (named[:1] > 0.5), 1.0, 0.0).astype(jnp.bfloat16)
+
+    def picked(rows):
+        return jnp.dot(pick, rows, preferred_element_type=jnp.float32).astype(jnp.bfloat16)
+
+    def scaled(rows):
+        return (rows.astype(jnp.float32) * weight).astype(jnp.bfloat16)
+
+    extra = first_width - META_LANES - width
+    inputs_ref[...] = picked(first_ref[:, :width])
+    grads_ref[:, :extra] = picked(scaled(first_ref[:, width : width + extra]))
+    grads_ref[:, extra:] = picked(scaled(second_ref[...]))
+
+
+def pick_rows(expert, topk, first_all, second_all, capacity, width):
+    devices, tokens, first_width = first_all.shape
+    second_width = second_all.shape[2]
+    out = jax.ShapeDtypeStruct((devices * capacity, width), first_all.dtype)
+    return pl.pallas_call(
+        pick_kernel,
+        grid_spec=pltpu.PrefetchScalarGridSpec(
+            num_scalar_prefetch=1,
+            grid=(devices,),
+            in_specs=[
+                pl.BlockSpec((None, tokens, first_width), lambda d, e: (d, 0, 0)),
+                pl.BlockSpec((None, tokens, second_width), lambda d, e: (d, 0, 0)),
+            ],
+            out_specs=[pl.BlockSpec((capacity, width), lambda d, e: (d, 0))] * 2,
+        ),
+        out_shape=(out, out),
+        compiler_params=pltpu.CompilerParams(vmem_limit_bytes=24 * 2**20),
+    )(jnp.stack([expert, jnp.int32(topk)]), first_all, second_all)
 
 
 def slot_ranks(named):
@@ -389,35 +453,46 @@
         cols == 2
         and inner_product % cols == 0
         and w_gate.shape[0] == 1
+        and experts_all <= 256
+        and 4 * topk <= META_LANES
         and 2 * devices * hidden.size * hidden.dtype.itemsize <= GATHER_LIMIT
     )
     if gather_plan:
-        meta = jnp.concatenate(
-            [expert_ids.astype(jnp.float32).T, gate_weights.T], axis=0
-        )
-        meta_all = lax.all_gather(meta, ("grp", "inner"), axis=0, tiled=True).reshape(
-            devices, 2, topk, token_rows
-        )
-        normed_all, upstream_all, head_query, head_output, head_key, head_value = spread(
-            normed, grad_out, queries, attn_out, keys, values, devices, inner_product, cols
+        high = lax.reduce_precision(gate_weights, 8, 7)
+        middle = lax.reduce_precision(gate_weights - high, 8, 7)
+        low = gate_weights - high - middle
+        extra = width // 4
+        blank = jnp.zeros((token_rows, META_LANES - 4 * topk), jnp.bfloat16)
+        first = jnp.concatenate(
+            [
+                normed,
+                grad_out[:, :extra],
+                expert_ids.astype(jnp.bfloat16),
+                high.astype(jnp.bfloat16),
+                middle.astype(jnp.bfloat16),
+                low.astype(jnp.bfloat16),
+                blank,
+            ],
+            axis=1,
+        )
+        first_all, second_all, head_query, head_output, head_key, head_value = spread(
+            first,
+            grad_out[:, extra:],
+            queries,
+            attn_out,
+            keys,
+            values,
+            devices,
+            inner_product,
+            cols,
         )
         expert = lax.axis_index("grp") * inner_product + lax.axis_index("inner")
-        chosen = meta_all[:, 0].astype(jnp.int32) == expert
-        named = jnp.any(chosen, axis=1)
-        weight = jnp.sum(jnp.where(chosen, meta_all[:, 1], 0.0), axis=1)
-        pick = (
-            jnp.arange(capacity, dtype=jnp.int32)[None, :, None] == slot_ranks(named)[:, None, :]
-        ) & named[:, None, :]
-        slot_weight = jnp.sum(jnp.where(pick, weight[:, None, :], 0.0), axis=2)
-        pick = pick.astype(jnp.bfloat16)
-        slot_inputs = jnp.einsum("dct,dtw->dcw", pick, normed_all)
-        slot_grads = jnp.einsum(
-            "dct,dtw->dcw", pick, upstream_all, preferred_element_type=jnp.float32
-        )
-        slot_grads = (slot_grads * slot_weight[:, :, None]).astype(jnp.bfloat16)
+        slot_inputs, slot_grads = pick_rows(
+            expert, topk, first_all, second_all, capacity, width
+        )
         returned = lax.all_to_all(
             expert_rows_grads(
-                slot_inputs.reshape(-1, width), slot_grads.reshape(-1, width), w_gate[0], w_up[0], w_down[0]
+                slot_inputs, slot_grads, w_gate[0], w_up[0], w_down[0]
             ),
             ("grp", "inner"),
             split_axis=0,

time: 614 us -> 568 us (0.925)
  blocking collectives: 71.2 us -> 0 us
  Pallas kernels: 168 us -> 197 us
  matrix products: 86.6 us -> 69.1 us
  starting transfers between devices: 12.8 us -> 23.2 us
    all_gather x1 -> x0, blocking collectives: 71.2 us -> none  [per_device(): lax.all_gather(meta, ('grp', 'inner'), axis=0, tiled=True)]
    pallas_call x0 -> x1, Pallas kernels: none -> 28.3 us  [pick_rows(): pl.pallas_call(pick_kernel, grid_spec=pltpu.PrefetchScalarGridSpec(num_sc...]
    dot_general x2 -> x0, matrix products: 16.3 us -> none  [the longest x1 8.23 us: per_device(): jnp.einsum('dct,dtw->dcw', pick, upstream_all, preferred_element_type=jnp...]
    all_to_all x1, starting transfers between devices: 4.13 us -> 14.7 us  [per_device(): lax.all_to_all(expert_rows_grads(slot_inputs, slot_grads, w_gate[0], w_up...]
    unnamed x71 -> x68, local copies, waits for them, and re-layouts: 23.7 us -> 19.2 us
  transfers between devices with their start and end apart: 4 -> 4, of which waited for: 4 -> 4; matrix products, arithmetic and copies ran while one was open for 5% -> 6% of each run, Pallas kernels for 0% -> 0%
where the time goes in v2:
time: 568 us; the launch traced here: 558 us
  Pallas kernels  197 us (35%)
  waiting for transfers between devices  195 us (34%)
  matrix products  69.1 us (12%)
  local copies, waits for them, and re-layouts  44.1 us (8%)
  starting transfers between devices  23.2 us (4%)
  other arithmetic  15.1 us (3%)
  between operations  14.7 us (3%)
    pallas_call x1, Pallas kernels, spread(): pl.pallas_call(functools.partial(spread_kernel, cols, peers // cols), out...  169 us
    all_to_all x1, waiting for transfers between devices, per_device(): lax.all_to_all(expert_rows_grads(slot_inputs, slot_grads, w_gate[0], w_up...  117 us
    all_gather x1, waiting for transfers between devices, per_device(): lax.all_gather(grad_resid, 'inner', axis=0, tiled=True)  54.2 us
    dot_general x8, matrix products, contract_last(): lax.dot_general(left, right, (((1,), (1,)), ((), ())), preferred_element_...  42.8 us
    pallas_call x1, Pallas kernels, pick_rows(): pl.pallas_call(pick_kernel, grid_spec=pltpu.PrefetchScalarGridSpec(num_sc...  28.3 us
    unnamed x68, local copies, waits for them, and re-layouts  19.2 us
    all_to_all x1, waiting for transfers between devices, per_device(): lax.all_to_all(grad_query_heads.astype(jnp.bfloat16), 'inner', split_axis...  15.8 us
    all_to_all x1, starting transfers between devices, per_device(): lax.all_to_all(expert_rows_grads(slot_inputs, slot_grads, w_gate[0], w_up...  14.7 us
  transfers between devices with their start and end apart: 4, of which 4 were waited for; matrix products, arithmetic and copies ran while one was open for 6% of the time, Pallas kernels for 0%

profile of v2, /device:TPU:0, one launch (start us, length us, event | category | flops | bytes accessed | tf_op | source)
XLA Modules:
  0.0 558.2 jit_solution(1632905042088492084)
XLA Ops:
  9.5 1.6 slice.104
  17.8 2.0 fusion.30
  20.5 2.0 concatenate.26.first_ref
  27.9 168.8 %shard_map.175 = (bf16[32,128,2688]{2,1,0:T(8,128)(2,1)S(1)}, bf16[32,128,1536]{2,1,0:T(8,128)(2,1)S(1)}, bf16[1024,512]{1,0:T(8,128)(2,1)S(1)}, bf16[1024,512]{...) custom-call(bf16[128,2688]{1,0:T(8,128)(2,1)S(1)} %copy-done.3, ...), custom_call_target="tpu_custom_call" | custom-call | bytes 524288000 | tf_op jit(solution)/shard_map/pallas_call | solution.py:329
  196.7 7.3 %copy-done.2 = bf16[32,128,2688]{2,1,0:T(8,128)(2,1)} copy-done((bf16[32,128,2688]{2,1,0:T(8,128)(2,1)}, bf16[32,128,2688]{2,1,0:T(8,128)(2,1)S(1)}, u32[]{:S(2)}) %copy-start.2) | copy-done | bytes 22020120
  204.8 28.3 %shard_map.176 = (bf16[1280,2048]{1,0:T(8,128)(2,1)S(1)}, bf16[1280,2048]{1,0:T(8,128)(2,1)S(1)}) custom-call(s32[2]{0:T(128)S(1)} %pad_add_fusion.expert_ref, bf16[32,128,2688]{2,1,0:T(8,128)(2,1)} %copy-done.2, bf16[32,128,1536]{2,1,0:T(8,128)(2,1)S(1)} %get-tuple-element.77.second_ref), custom_call_target="tpu_custom_call" | custom-call | tf_op jit(solution)/shard_map/pallas_call | solution.py:400
  233.1 4.3 fusion.8
  237.5 4.4 fusion.12
  241.9 5.4 fusion.5
  247.3 7.4 %fusion.6 = f32[1280,2048]{1,0:T(8,128)} fusion(bf16[1280,768]{1,0:T(8,128)(2,1)S(1)} %fusion.5, bf16[1,2048,768]{2,1,0:T(8,128)(2,1)S(1)} %copy-done), kind=kOutput, calls=%fused_computation.15 | convolution fusion | flops 4026531840 | bytes 15597568 | tf_op jit(solution)/shard_map/dot_general | solution.py:18
  254.7 10.1 %add_convert_fusion = bf16[1280,2048]{1,0:T(8,128)(2,1)} fusion(f32[1280,2048]{1,0:T(8,128)} %fusion.6, bf16[1,2048,768]{2,1,0:T(8,128)(2,1)S(1)} %copy-done.27, f32[1280,768]{1,0:T(8,128)} %copy-done.29, f32[1280,768]{1,0:T(8,128)S(1)} %fusion.8), kind=kOutput, calls=%fused_computation | convolution fusion | flops 4037672960 | bytes 26738688 | tf_op jit(solution)/shard_map/dot_general | solution.py:18
  264.8 14.7 %all-to-all-start = ((bf16[32,40,2048]{2,1,0:T(8,128)(2,1)}), bf16[32,40,2048]{2,1,0:T(8,128)(2,1)}, u32[]{:S(2)}, u32[]{:S(2)}) async-start(bf16[32,40,2048]{2,1,0:T(8,128)(2,1)} %bitcast.57), calls=%async_computation | async-start | bytes 10485760 | tf_op jit(solution)/shard_map/all_to_all | solution.py:493
  279.8 117.3 %all-to-all-done = bf16[32,40,2048]{2,1,0:T(8,128)(2,1)} async-done(((bf16[32,40,2048]{2,1,0:T(8,128)(2,1)}), bf16[32,40,2048]{2,1,0:T(8,128)(2,1)}, u32[]{:S(2)}, u32[]{:S(2)}) %all-to-all-start) | async-done | bytes 5242912 | tf_op jit(solution)/shard_map/all_to_all | solution.py:493
  397.1 3.5 fusion.36
  404.7 2.2 reshape.190
  409.9 4.1 exponential_select_fusion.1
  414.0 4.5 fusion.63
  418.6 54.2 %all-gather.2.cloned.1.call-done = bf16[1024,2048]{1,0:T(8,128)(2,1)} async-done(((bf16[128,2048]{1,0:T(8,128)(2,1)}), bf16[1024,2048]{1,0:T(8,128)(2,1)}) %all-gather.2.cloned.1.call-update) | async-done | bytes 4194320 | tf_op jit(solution)/shard_map/all_gather | solution.py:579
  472.7 5.2 convolution_convert_fusion
  479.6 3.1 fusion.17
  486.6 1.7 multiply_reduce_fusion
  488.3 6.3 %multiply_convert_fusion = bf16[2048,1024]{1,0:T(8,128)(2,1)S(1)} fusion(f32[2048,1024]{1,0:T(8,128)} %fusion.63, bf16[2048,128]{1,0:T(8,128)(2,1)S(1)} %reshape.194, bf16[1024,128]{1,0:T(8,128)(2,1)S(1)} %copy-done.15, f32[2048]{0:T(1024)S(1)} %multiply_reduce_fusion, f32[2048]{0:T(1024)S(1)} %sub.69, s32[2048]{0:T(1024)S(1)} %broadcast_add_fusion), kind=kOutput, calls=%fused_computation.1 | convolution fusion | flops 551550976 | bytes 13393920 | tf_op jit(solution)/shard_map/dot_general | solution.py:18
  494.7 3.0 fusion.26
  499.9 4.1 all-to-all-start.2
  505.1 3.4 fusion.16
  509.9 7.7 %all-to-all-done.2 = bf16[8,128,256]{2,1,0:T(8,128)(2,1)} async-done(((bf16[8,128,256]{2,1,0:T(8,128)(2,1)}), bf16[8,128,256]{2,1,0:T(8,128)(2,1)}, u32[]{:S(2)}, u32[]{:S(2)}) %all-to-all-start.2) | async-done | bytes 524320 | tf_op jit(solution)/shard_map/all_to_all | solution.py:624
  517.6 4.2 all-to-all-start.1
  521.9 2.1 convert_element_type.123
  524.0 2.0 reduce.10
  530.9 15.8 %all-to-all-done.1 = bf16[8,128,512]{2,1,0:T(8,128)(2,1)} async-done(((bf16[8,128,512]{2,1,0:T(8,128)(2,1)}), bf16[8,128,512]{2,1,0:T(8,128)(2,1)}, u32[]{:S(2)}, u32[]{:S(2)}) %all-to-all-start.1) | async-done | bytes 1048608 | tf_op jit(solution)/shard_map/all_to_all | solution.py:621
  546.7 2.3 copy.61
  548.9 2.3 copy.64
  (110 shorter events, 38.1 us)
Async XLA Ops:
  7.2 225.9 %copy-start = (bf16[1,2048,768]{2,1,0:T(8,128)(2,1)S(1)}, bf16[1,2048,768]{2,1,0:T(8,128)(2,1)}, u32[]{:S(2)}) copy-start(bf16[1,2048,768]{2,1,0:T(8,128)(2,1)} %param.31) | copy-start | bytes 9437188
  22.5 1.1 copy-start.3
  23.6 1.2 copy-start.8
  24.8 1.2 copy-start.9
  196.7 7.3 %copy-start.2 = (bf16[32,128,2688]{2,1,0:T(8,128)(2,1)}, bf16[32,128,2688]{2,1,0:T(8,128)(2,1)S(1)}, u32[]{:S(2)}) copy-start(bf16[32,128,2688]{2,1,0:T(8,128)(2,1)S(1)} %get-tuple-element.76.first_ref) | copy-start | bytes 66060292
  204.8 28.3 %copy-start.4 = (bf16[1024,512]{1,0:T(8,128)(2,1)}, bf16[1024,512]{1,0:T(8,128)(2,1)S(1)}, u32[]{:S(2)}) copy-start(bf16[1024,512]{1,0:T(8,128)(2,1)S(1)} %get-tuple-element.80) | copy-start | bytes 3145732
  204.8 28.3 %copy-start.6 = (bf16[1024,512]{1,0:T(8,128)(2,1)}, bf16[1024,512]{1,0:T(8,128)(2,1)S(1)}, u32[]{:S(2)}) copy-start(bf16[1024,512]{1,0:T(8,128)(2,1)S(1)} %get-tuple-element.83) | copy-start | bytes 3145732
  204.8 28.3 %copy-start.14 = (bf16[1024,128]{1,0:T(8,128)(2,1)}, bf16[1024,128]{1,0:T(8,128)(2,1)S(1)}, u32[]{:S(2)}) copy-start(bf16[1024,128]{1,0:T(8,128)(2,1)S(1)} %get-tuple-element.82) | copy-start | bytes 786436
  233.1 4.3 copy-start.26
  237.5 4.4 copy-start.27
  241.9 5.4 copy-start.29
  264.8 14.8 %copy-start.25 = (s32[128,8]{0,1:T(8,128)S(1)}, s32[128,8]{0,1:T(8,128)}, u32[]{:S(2)}) copy-start(s32[128,8]{0,1:T(8,128)} %param.29) | copy-start | bytes 12292
  264.8 132.3 %copy-start.17 = (bf16[128,2048]{1,0:T(8,128)(2,1)S(1)}, bf16[128,2048]{1,0:T(8,128)(2,1)}, u32[]{:S(2)}) copy-start(bf16[128,2048]{1,0:T(8,128)(2,1)} %param.27) | copy-start | bytes 1572868
  264.8 132.3 %copy-start.23 = (f32[2048]{0:T(1024)S(1)}, f32[2048]{0:T(1024)}, u32[]{:S(2)}) copy-start(f32[2048]{0:T(1024)} %param.28) | copy-start | bytes 24580
  264.8 132.3 %all-to-all-start = ((bf16[32,40,2048]{2,1,0:T(8,128)(2,1)}), bf16[32,40,2048]{2,1,0:T(8,128)(2,1)}, u32[]{:S(2)}, u32[]{:S(2)}) async-start(bf16[32,40,2048]{2,1,0:T(8,128)(2,1)} %bitcast.57), calls=%async_computation | async-start | bytes 10485760 | tf_op jit(solution)/shard_map/all_to_all | solution.py:493
  279.6 121.0 %copy-start.20 = (bf16[128,2048]{1,0:T(8,128)(2,1)S(1)}, bf16[128,2048]{1,0:T(8,128)(2,1)}, u32[]{:S(2)}) copy-start(bf16[128,2048]{1,0:T(8,128)(2,1)} %param.26) | copy-start | bytes 1572868
  279.6 193.2 %all-gather.2.cloned.1.call-start = ((), (), s32[]{:S(2)}) async-start(), calls=%async_computation.3 | async-start | bytes 4718592 | tf_op jit(solution)/shard_map/all_gather | solution.py:579
  279.8 122.0 %copy-start.5 = (bf16[1024,512]{1,0:T(8,128)(2,1)S(1)}, bf16[1024,512]{1,0:T(8,128)(2,1)}, u32[]{:S(2)}) copy-start(bf16[1024,512]{1,0:T(8,128)(2,1)} %copy-done.4) | copy-start | bytes 3145732
  279.8 122.0 %copy-start.7 = (bf16[1024,512]{1,0:T(8,128)(2,1)S(1)}, bf16[1024,512]{1,0:T(8,128)(2,1)}, u32[]{:S(2)}) copy-start(bf16[1024,512]{1,0:T(8,128)(2,1)} %copy-done.6) | copy-start | bytes 3145732
  401.8 5.0 copy-start.24
  403.3 6.6 %copy-start.11 = (bf16[1024,128]{1,0:T(8,128)(2,1)S(1)}, bf16[1024,128]{1,0:T(8,128)(2,1)}, u32[]{:S(2)}) copy-start(bf16[1024,128]{1,0:T(8,128)(2,1)} %copy-done.10) | copy-start | bytes 786436
  409.6 9.0 %copy-start.18 = (bf16[2048,128]{1,0:T(8,128)(2,1)}, bf16[2048,128]{1,0:T(8,128)(2,1)S(1)}, u32[]{:S(2)}) copy-start(bf16[2048,128]{1,0:T(8,128)(2,1)S(1)} %reshape.193) | copy-start | bytes 1572868
  479.2 3.5 copy-start.15
  479.2 3.5 copy-start.16
  486.5 8.1 %slice-start = ((s8[8388608]{0:T(1024)(128)(4,1)}), s8[4194304]{0:T(1024)(128)(4,1)S(1)}, s32[]{:S(2)}) async-start(s8[8388608]{0:T(1024)(128)(4,1)} %bitcast.55), calls=%async_computation.4 | async-start | bytes 8388608
  488.3 6.4 %slice-start.1 = ((s8[8388608]{0:T(1024)(128)(4,1)}), s8[4194304]{0:T(1024)(128)(4,1)S(1)}, s32[]{:S(2)}) async-start(s8[8388608]{0:T(1024)(128)(4,1)} %bitcast.55), calls=%async_computation.5 | async-start | bytes 8388608
  494.7 3.0 copy-start.28
  494.7 3.0 copy-start.19
  494.7 3.0 copy-start.22
  499.9 17.7 %all-to-all-start.2 = ((bf16[8,128,256]{2,1,0:T(8,128)(2,1)}), bf16[8,128,256]{2,1,0:T(8,128)(2,1)}, u32[]{:S(2)}, u32[]{:S(2)}) async-start(bf16[8,128,256]{2,1,0:T(8,128)(2,1)} %pad_maximum_fusion.1), calls=%async_computation.2 | async-start | bytes 1048576 | tf_op jit(solution)/shard_map/all_to_all | solution.py:624
  517.6 29.0 %all-to-all-start.1 = ((bf16[8,128,512]{2,1,0:T(8,128)(2,1)}), bf16[8,128,512]{2,1,0:T(8,128)(2,1)}, u32[]{:S(2)}, u32[]{:S(2)}) async-start(bf16[8,128,512]{2,1,0:T(8,128)(2,1)} %bitcast.8), calls=%async_computation.1 | async-start | bytes 2097152 | tf_op jit(solution)/shard_map/all_to_all | solution.py:621
  521.9 29.3 %copy-start.1 = (bf16[1,2048,768]{2,1,0:T(8,128)(2,1)S(1)}, bf16[1,2048,768]{2,1,0:T(8,128)(2,1)}, u32[]{:S(2)}) copy-start(bf16[1,2048,768]{2,1,0:T(8,128)(2,1)} %param.31) | copy-start | bytes 9437188
  (4 other events, 3.6 us)
Sparse Core Ops, SparseCore 0:
  401.9 70.7 all-gather.1

commit v3 on v2

--- a/solution.py
+++ b/solution.py
@@ -35,8 +35,14 @@
         jnp.bfloat16
     )
     grad_up = (back_hidden * gate_pre * sigmoid).astype(jnp.bfloat16)
-    grad_in = contract_last(grad_gate, gate_matrix) + contract_last(grad_up, up_matrix)
-    return grad_in.astype(jnp.bfloat16)
+    half = gate_matrix.shape[0] // 2
+
+    def columns(gate_rows, up_rows):
+        grad_in = contract_last(grad_gate, gate_rows) + contract_last(grad_up, up_rows)
+        return grad_in.astype(jnp.bfloat16)
+
+    first = columns(gate_matrix[:half], up_matrix[:half])
+    return first, columns(gate_matrix[half:], up_matrix[half:])
 
 
 def expert_grads(received, w_gate, w_up, w_down):
@@ -344,7 +350,7 @@
             pltpu.SemaphoreType.DMA((8,)),
         ],
         compiler_params=pltpu.CompilerParams(
-            collective_id=0, has_side_effects=True, vmem_limit_bytes=8 * 2**20
+            collective_id=0, has_side_effects=True, vmem_limit_bytes=56 * 2**20
         ),
         cost_estimate=pl.CostEstimate(
             flops=0, bytes_accessed=500 * 2**20, transcendentals=0
@@ -409,7 +415,7 @@
             out_specs=[pl.BlockSpec((capacity, width), lambda d, e: (d, 0))] * 2,
         ),
         out_shape=(out, out),
-        compiler_params=pltpu.CompilerParams(vmem_limit_bytes=24 * 2**20),
+        compiler_params=pltpu.CompilerParams(vmem_limit_bytes=56 * 2**20),
     )(jnp.stack([expert, jnp.int32(topk)]), first_all, second_all)
 
 
@@ -490,15 +496,13 @@
         slot_inputs, slot_grads = pick_rows(
             expert, topk, first_all, second_all, capacity, width
         )
-        returned = lax.all_to_all(
-            expert_rows_grads(
-                slot_inputs, slot_grads, w_gate[0], w_up[0], w_down[0]
-            ),
-            ("grp", "inner"),
-            split_axis=0,
-            concat_axis=0,
-            tiled=True,
-        )
+        row_parts = expert_rows_grads(
+            slot_inputs, slot_grads, w_gate[0], w_up[0], w_down[0]
+        )
+        returned = [
+            lax.all_to_all(part, ("grp", "inner"), split_axis=0, concat_axis=0, tiled=True)
+            for part in row_parts
+        ]
         mine = jnp.any(
             expert_ids.T[None] == jnp.arange(experts_all, dtype=jnp.int32)[:, None, None], axis=1
         )
@@ -509,8 +513,9 @@
             )
             & mine[:, None, :]
         ).astype(jnp.bfloat16)
-        grad_normed = contract_first(
-            place.reshape(experts_all * capacity, token_rows), returned
+        place = place.reshape(experts_all * capacity, token_rows)
+        grad_normed = jnp.concatenate(
+            [contract_first(place, part) for part in returned], axis=1
         )
     else:
         flat_count = token_rows * topk

time: 568 us -> 557 us (0.981)
  local copies, waits for them, and re-layouts: 44.1 us -> 25.2 us
  Pallas kernels: 197 us -> 203 us
    unnamed x68, local copies, waits for them, and re-layouts: 19.2 us -> 5.16 us
    all_to_all x1 -> x2, waiting for transfers between devices: 117 us -> 112 us  [per_device(): lax.all_to_all(part, ('grp', 'inner'), split_axis=0, concat_axis=0, tiled...]
    all_to_all x1 -> x2, starting transfers between devices: 14.7 us -> 18 us  [per_device(): lax.all_to_all(part, ('grp', 'inner'), split_axis=0, concat_axis=0, tiled...]
    dot_general x8 -> x10, matrix products: 42.8 us -> 40.8 us  [contract_last(): lax.dot_general(left, right, (((1,), (1,)), ((), ())), preferred_element_...]
    dot_general x5 -> x6, matrix products: 12.3 us -> 13.2 us  [contract_first(): lax.dot_general(left, right, (((0,), (0,)), ((), ())), preferred_element_...]
  transfers between devices with their start and end apart: 4 -> 5, of which waited for: 4 -> 5; matrix products, arithmetic and copies ran while one was open for 6% -> 7% of each run, Pallas kernels for 0% -> 0%
where the time goes in v3:
time: 557 us; the launch traced here: 552 us
  Pallas kernels  203 us (36%)
  waiting for transfers between devices  195 us (35%)
  matrix products  72 us (13%)
  starting transfers between devices  26.4 us (5%)
  local copies, waits for them, and re-layouts  25.2 us (5%)
  other arithmetic  15.6 us (3%)
  between operations  14.9 us (3%)
    pallas_call x1, Pallas kernels, spread(): pl.pallas_call(functools.partial(spread_kernel, cols, peers // cols), out...  170 us
    all_to_all x2, waiting for transfers between devices, per_device(): lax.all_to_all(part, ('grp', 'inner'), split_axis=0, concat_axis=0, tiled...  112 us
    all_gather x1, waiting for transfers between devices, per_device(): lax.all_gather(grad_resid, 'inner', axis=0, tiled=True)  59.2 us
    dot_general x10, matrix products, contract_last(): lax.dot_general(left, right, (((1,), (1,)), ((), ())), preferred_element_...  40.8 us
    pallas_call x1, Pallas kernels, pick_rows(): pl.pallas_call(pick_kernel, grid_spec=pltpu.PrefetchScalarGridSpec(num_sc...  32.6 us
    all_to_all x2, starting transfers between devices, per_device(): lax.all_to_all(part, ('grp', 'inner'), split_axis=0, concat_axis=0, tiled...  18 us
    all_to_all x1, waiting for transfers between devices, per_device(): lax.all_to_all(grad_query_heads.astype(jnp.bfloat16), 'inner', split_axis...  15.8 us
    dot_general x6, matrix products, contract_first(): lax.dot_general(left, right, (((0,), (0,)), ((), ())), preferred_element_...  13.2 us
  transfers between devices with their start and end apart: 5, of which 5 were waited for; matrix products, arithmetic and copies ran while one was open for 7% of the time, Pallas kernels for 0%

profile of v3, /device:TPU:0, one launch (start us, length us, event | category | flops | bytes accessed | tf_op | source)
XLA Modules:
  0.0 551.9 jit_solution(2943308239505694123)
XLA Ops:
  13.9 2.0 fusion.35
  18.4 170.1 %shard_map.175 = (bf16[32,128,2688]{2,1,0:T(8,128)(2,1)}, bf16[32,128,1536]{2,1,0:T(8,128)(2,1)}, bf16[1024,512]{1,0:T(8,128)(2,1)}, bf16[1024,512]{1,0:T(8,128)...) custom-call(bf16[128,2688]{1,0:T(8,128)(2,1)} %concatenate.29.first_ref, ...), custom_call_target="tpu_custom_call" | custom-call | bytes 524288000 | tf_op jit(solution)/shard_map/pallas_call | solution.py:335
  188.6 32.6 %shard_map.176 = (bf16[1280,2048]{1,0:T(8,128)(2,1)}, bf16[1280,2048]{1,0:T(8,128)(2,1)}) custom-call(s32[2]{0:T(128)} %pad_add_fusion.expert_ref, bf16[32,128,2688]{2,1,0:T(8,128)(2,1)} %get-tuple-element.76.first_ref, bf16[32,128,1536]{2,1,0:T(8,128)(2,1)} %get-tuple-element.77.second_ref), custom_call_target="tpu_custom_call" | custom-call | tf_op jit(solution)/shard_map/pallas_call | solution.py:406
  221.2 6.3 %fusion.6 = f32[1280,768]{1,0:T(8,128)S(1)} fusion(bf16[1280,2048]{1,0:T(8,128)(2,1)} %get-tuple-element.79, bf16[1,2048,768]{2,1,0:T(8,128)(2,1)S(1)} %copy-done.21), kind=kOutput, calls=%fused_computation.16 | convolution fusion | flops 4026531840 | bytes 12320768 | tf_op jit(solution)/shard_map/dot_general | solution.py:30
  227.5 6.7 %multiply_convert_fusion.2 = (bf16[1280,768]{1,0:T(8,128)(2,1)S(1)}, f32[1280,768]{1,0:T(8,128)}) fusion(f32[1280,768]{1,0:T(8,128)S(1)} %fusion.6, bf16[1280,2048]{1,0:T(8,128)(2,1)S(1)} %copy-done.20, bf16[1,768,2048]{2,1,0:T(8,128)(2,1)S(1)} %copy-done), kind=kOutput, calls=%fused_computation.13 | convolution fusion | flops 4032430080 | bytes 18219008 | tf_op jit(solution)/shard_map/dot_general | solution.py:18
  234.2 7.4 %fusion.5 = bf16[1280,768]{1,0:T(8,128)(2,1)S(1)} fusion(f32[1280,768]{1,0:T(8,128)S(1)} %fusion.6, f32[1280,768]{1,0:T(8,128)} %get-tuple-element.111, bf16[1280,2048]{1,0:T(8,128)(2,1)S(1)} %bitcast.82, bf16[1,2048,768]{2,1,0:T(8,128)(2,1)S(1)} %copy-done.22), kind=kOutput, calls=%fused_computation.15 | convolution fusion | flops 4036362240 | bytes 18219008 | tf_op jit(solution)/shard_map/dot_general | solution.py:31
  241.6 2.3 fusion.19
  243.9 3.8 add_convert_fusion.1
  247.7 14.3 %all-to-all-start = ((bf16[32,40,1024]{2,1,0:T(8,128)(2,1)}), bf16[32,40,1024]{2,1,0:T(8,128)(2,1)S(1)}, u32[]{:S(2)}, u32[]{:S(2)}) async-start(bf16[32,40,1024]{2,1,0:T(8,128)(2,1)} %bitcast.74), calls=%async_computation | async-start | bytes 5242880 | tf_op jit(solution)/shard_map/all_to_all | solution.py:503
  262.1 4.4 fusion.16
  266.5 3.9 add_convert_fusion
  270.4 52.9 %all-to-all-done = bf16[32,40,1024]{2,1,0:T(8,128)(2,1)S(1)} async-done(((bf16[32,40,1024]{2,1,0:T(8,128)(2,1)}), bf16[32,40,1024]{2,1,0:T(8,128)(2,1)S(1)}, u32[]{:S(2)}, u32[]{:S(2)}) %all-to-all-start) | async-done | bytes 2621472 | tf_op jit(solution)/shard_map/all_to_all | solution.py:503
  323.2 3.7 all-to-all-start.1
  328.6 59.6 %all-to-all-done.1 = bf16[32,40,1024]{2,1,0:T(8,128)(2,1)} async-done(((bf16[32,40,1024]{2,1,0:T(8,128)(2,1)}), bf16[32,40,1024]{2,1,0:T(8,128)(2,1)}, u32[]{:S(2)}, u32[]{:S(2)}) %all-to-all-start.1) | async-done | bytes 2621472 | tf_op jit(solution)/shard_map/all_to_all | solution.py:503
  388.1 2.3 convolution_bitcast_fusion
  398.3 2.9 exponential_select_fusion.1
  401.2 4.5 fusion.70
  405.7 59.2 %all-gather.2.cloned.1.call-done = bf16[1024,2048]{1,0:T(8,128)(2,1)} async-done(((bf16[128,2048]{1,0:T(8,128)(2,1)}), bf16[1024,2048]{1,0:T(8,128)(2,1)}) %all-gather.2.cloned.1.call-update) | async-done | bytes 4194320 | tf_op jit(solution)/shard_map/all_gather | solution.py:584
  464.9 5.2 convolution_convert_fusion
  471.7 3.8 fusion.13
  478.0 2.2 reshape.200
  481.7 6.5 %multiply_convert_fusion = bf16[2048,1024]{1,0:T(8,128)(2,1)S(1)} fusion(f32[2048,1024]{1,0:T(8,128)} %fusion.70, bf16[2048,128]{1,0:T(8,128)(2,1)} %reshape.200, bf16[1024,128]{1,0:T(8,128)(2,1)} %get-tuple-element.82, f32[2048]{0:T(1024)S(1)} %multiply_reduce_fusion, f32[2048]{0:T(1024)S(1)} %sub.69, s32[2048]{0:T(1024)S(1)} %broadcast_add_fusion), kind=kOutput, calls=%fused_computation | convolution fusion | flops 551550976 | bytes 13393920 | tf_op jit(solution)/shard_map/dot_general | solution.py:18
  488.3 3.0 fusion.31
  493.5 4.2 all-to-all-start.3
  498.7 3.4 fusion.12
  503.5 7.7 %all-to-all-done.3 = bf16[8,128,256]{2,1,0:T(8,128)(2,1)} async-done(((bf16[8,128,256]{2,1,0:T(8,128)(2,1)}), bf16[8,128,256]{2,1,0:T(8,128)(2,1)}, u32[]{:S(2)}, u32[]{:S(2)}) %all-to-all-start.3) | async-done | bytes 524320 | tf_op jit(solution)/shard_map/all_to_all | solution.py:629
  511.2 4.2 all-to-all-start.2
  515.5 2.1 convert_element_type.127
  517.6 2.0 reduce.10
  524.5 15.8 %all-to-all-done.2 = bf16[8,128,512]{2,1,0:T(8,128)(2,1)} async-done(((bf16[8,128,512]{2,1,0:T(8,128)(2,1)}), bf16[8,128,512]{2,1,0:T(8,128)(2,1)}, u32[]{:S(2)}, u32[]{:S(2)}) %all-to-all-start.2) | async-done | bytes 1048608 | tf_op jit(solution)/shard_map/all_to_all | solution.py:626
  540.2 2.3 copy.61
  542.5 2.3 copy.64
  (117 shorter events, 33.7 us)
Async XLA Ops:
  7.2 220.3 %copy-start = (bf16[1,768,2048]{2,1,0:T(8,128)(2,1)S(1)}, bf16[1,768,2048]{2,1,0:T(8,128)(2,1)}, u32[]{:S(2)}) copy-start(bf16[1,768,2048]{2,1,0:T(8,128)(2,1)} %param.33) | copy-start | bytes 9437188
  188.6 32.6 %copy-start.21 = (bf16[1,2048,768]{2,1,0:T(8,128)(2,1)S(1)}, bf16[1,2048,768]{2,1,0:T(8,128)(2,1)}, u32[]{:S(2)}) copy-start(bf16[1,2048,768]{2,1,0:T(8,128)(2,1)} %param.31) | copy-start | bytes 9437188
  221.2 6.3 %copy-start.20 = (bf16[1280,2048]{1,0:T(8,128)(2,1)S(1)}, bf16[1280,2048]{1,0:T(8,128)(2,1)}, u32[]{:S(2)}) copy-start(bf16[1280,2048]{1,0:T(8,128)(2,1)} %get-tuple-element.78) | copy-start | bytes 15728644
  221.2 13.0 %slice-start.2 = ((s8[5242880]{0:T(1024)(128)(4,1)}), s8[4194304]{0:T(1024)(128)(4,1)S(1)}, s32[]{:S(2)}) async-start(s8[5242880]{0:T(1024)(128)(4,1)} %bitcast.81), calls=%async_computation.7 | async-start | bytes 8388608
  227.5 6.7 %slice-start.3 = ((s8[5242880]{0:T(1024)(128)(4,1)}), s8[1048576]{0:T(1024)(128)(4,1)S(1)}, s32[]{:S(2)}) async-start(s8[5242880]{0:T(1024)(128)(4,1)} %bitcast.81), calls=%async_computation.8 | async-start | bytes 2097152
  227.5 6.7 %copy-start.22 = (bf16[1,2048,768]{2,1,0:T(8,128)(2,1)S(1)}, bf16[1,2048,768]{2,1,0:T(8,128)(2,1)}, u32[]{:S(2)}) copy-start(bf16[1,2048,768]{2,1,0:T(8,128)(2,1)} %param.32) | copy-start | bytes 9437188
  234.2 9.7 %copy-start.26 = (bf16[1280,768]{1,0:T(8,128)(2,1)}, bf16[1280,768]{1,0:T(8,128)(2,1)S(1)}, u32[]{:S(2)}) copy-start(bf16[1280,768]{1,0:T(8,128)(2,1)S(1)} %get-tuple-element.110) | copy-start | bytes 5898244
  247.7 75.5 %all-to-all-start = ((bf16[32,40,1024]{2,1,0:T(8,128)(2,1)}), bf16[32,40,1024]{2,1,0:T(8,128)(2,1)S(1)}, u32[]{:S(2)}, u32[]{:S(2)}) async-start(bf16[32,40,1024]{2,1,0:T(8,128)(2,1)} %bitcast.74), calls=%async_computation | async-start | bytes 5242880 | tf_op jit(solution)/shard_map/all_to_all | solution.py:503
  262.0 4.4 copy-start.23
  262.1 4.4 copy-start.27
  270.4 56.6 %copy-start.19 = (s32[128,8]{0,1:T(8,128)S(1)}, s32[128,8]{0,1:T(8,128)}, u32[]{:S(2)}) copy-start(s32[128,8]{0,1:T(8,128)} %param.29) | copy-start | bytes 12292
  323.2 64.9 %all-to-all-start.1 = ((bf16[32,40,1024]{2,1,0:T(8,128)(2,1)}), bf16[32,40,1024]{2,1,0:T(8,128)(2,1)}, u32[]{:S(2)}, u32[]{:S(2)}) async-start(bf16[32,40,1024]{2,1,0:T(8,128)(2,1)} %bitcast.73), calls=%async_computation.1 | async-start | bytes 5242880 | tf_op jit(solution)/shard_map/all_to_all | solution.py:503
  326.9 63.5 %copy-start.3 = (bf16[128,2048]{1,0:T(8,128)(2,1)S(1)}, bf16[128,2048]{1,0:T(8,128)(2,1)}, u32[]{:S(2)}) copy-start(bf16[128,2048]{1,0:T(8,128)(2,1)} %param.27) | copy-start | bytes 1572868
  326.9 63.5 %copy-start.16 = (f32[2048]{0:T(1024)S(1)}, f32[2048]{0:T(1024)}, u32[]{:S(2)}) copy-start(f32[2048]{0:T(1024)} %param.28) | copy-start | bytes 24580
  326.9 137.9 %all-gather.2.cloned.1.call-start = ((), (), s32[]{:S(2)}) async-start(), calls=%async_computation.4 | async-start | bytes 4718592 | tf_op jit(solution)/shard_map/all_gather | solution.py:584
  328.6 63.2 %copy-start.4 = (f32[128,1024]{1,0:T(8,128)S(1)}, f32[128,1024]{1,0:T(8,128)}, u32[]{:S(2)}) copy-start(f32[128,1024]{1,0:T(8,128)} %convolution_bitcast_fusion.1) | copy-start | bytes 1572868
  328.6 63.2 %copy-start.9 = (bf16[128,2048]{1,0:T(8,128)(2,1)S(1)}, bf16[128,2048]{1,0:T(8,128)(2,1)}, u32[]{:S(2)}) copy-start(bf16[128,2048]{1,0:T(8,128)(2,1)} %param.26) | copy-start | bytes 1572868
  393.0 3.3 copy-start.18
  394.9 3.4 copy-start.13
  396.2 4.9 copy-start.11
  398.0 3.2 copy-start.7
  405.7 65.6 %copy-start.6 = (f32[2048,128]{1,0:T(8,128)S(1)}, f32[2048,128]{1,0:T(8,128)}, u32[]{:S(2)}) copy-start(f32[2048,128]{1,0:T(8,128)} %reshape.202) | copy-start | bytes 3145732
  471.7 3.8 copy-start.2
  471.7 3.8 copy-start.17
  476.5 3.6 copy-start.5
  480.1 8.1 %slice-start = ((s8[8388608]{0:T(1024)(128)(4,1)}), s8[4194304]{0:T(1024)(128)(4,1)S(1)}, s32[]{:S(2)}) async-start(s8[8388608]{0:T(1024)(128)(4,1)} %bitcast.70), calls=%async_computation.5 | async-start | bytes 8388608
  481.7 6.5 %slice-start.1 = ((s8[8388608]{0:T(1024)(128)(4,1)}), s8[4194304]{0:T(1024)(128)(4,1)S(1)}, s32[]{:S(2)}) async-start(s8[8388608]{0:T(1024)(128)(4,1)} %bitcast.70), calls=%async_computation.6 | async-start | bytes 8388608
  481.7 6.5 %copy-start.10 = (bf16[2048,128]{1,0:T(8,128)(2,1)S(1)}, bf16[2048,128]{1,0:T(8,128)(2,1)}, u32[]{:S(2)}) copy-start(bf16[2048,128]{1,0:T(8,128)(2,1)} %reshape.200) | copy-start | bytes 1572868
  481.7 6.5 %copy-start.14 = (f32[512,128]{1,0:T(8,128)S(1)}, f32[512,128]{1,0:T(8,128)}, u32[]{:S(2)}) copy-start(f32[512,128]{1,0:T(8,128)} %fusion.13) | copy-start | bytes 786436
  493.5 17.7 %all-to-all-start.3 = ((bf16[8,128,256]{2,1,0:T(8,128)(2,1)}), bf16[8,128,256]{2,1,0:T(8,128)(2,1)}, u32[]{:S(2)}, u32[]{:S(2)}) async-start(bf16[8,128,256]{2,1,0:T(8,128)(2,1)} %pad_maximum_fusion.1), calls=%async_computation.3 | async-start | bytes 1048576 | tf_op jit(solution)/shard_map/all_to_all | solution.py:629
  511.2 29.0 %all-to-all-start.2 = ((bf16[8,128,512]{2,1,0:T(8,128)(2,1)}), bf16[8,128,512]{2,1,0:T(8,128)(2,1)}, u32[]{:S(2)}, u32[]{:S(2)}) async-start(bf16[8,128,512]{2,1,0:T(8,128)(2,1)} %bitcast.14), calls=%async_computation.2 | async-start | bytes 2097152 | tf_op jit(solution)/shard_map/all_to_all | solution.py:626
  515.4 29.3 %copy-start.1 = (bf16[1,768,2048]{2,1,0:T(8,128)(2,1)S(1)}, bf16[1,768,2048]{2,1,0:T(8,128)(2,1)}, u32[]{:S(2)}) copy-start(bf16[1,768,2048]{2,1,0:T(8,128)(2,1)} %param.33) | copy-start | bytes 9437188
  (5 other events, 12.4 us)
Sparse Core Ops, SparseCore 0:
  393.1 71.7 all-gather.1
